TPU v7x, 128 devices: a whole 4x4x4 slice. The times are simulated.
128 devices in a mesh: blk: 8 (over x, z_hi), grp: 16 (over z_lo, y, core).
Axes of the slice: x: 4, y: 4, z: 4 (z_hi: 2, z_lo: 2; z = z_hi * 2 + z_lo), core: 2. Of those that a mesh axis runs over, the one named last changes fastest.
Arguments:
- incident: float32 [8, 16384, 240], P('blk', 'grp'), may hold values from -6 to 6
- mie_coef: float32 [8, 16384, 240], P('blk', 'grp'), may hold values from 0.15 to 0.45
- owner_dev: int32 [8, 49152, 1], P('blk', 'grp'), may hold values from 0 to 15; in each aligned block of 3072 rows (0 to 3071, 3072 to 6143, ..., all dimensions but the last counted through in order) at most 512 rows name the same one
- near_row: int32 [8, 49152], P('blk', 'grp'), may hold values from 0 to 1023
- table_id: int32 [8, 49152], P('blk', 'grp'), may hold values from 0 to 7
- tables: bfloat16 [8, 240, 240], replicated, may hold values from -0.4 to 0.6
- wave_out: bfloat16 [240, 512], replicated, may hold values from -0.375 to 0.375
- wave_in: bfloat16 [512, 240], replicated, may hold values from -0.25 to 0.25
- plane_angle: bfloat16 [8, 16384, 512], P('blk', 'grp'), may hold values from -3.140625 to 3.140625
- far_trans: float32 [8, 16, 8, 512], P('blk', 'grp'), may hold values from -0.0625 to 0.0625
Outputs:
- solution: float32 [8, 16384, 240], P('blk', 'grp')
- residual: float32 [8, 16384, 240], P('blk', 'grp')
- hessenberg: float32 [3, 2], replicated
Inputs may be any that keep to these rules, and one draw needn't show every extreme that they name: `owner_dev`: among the 3072 requests of one device, at most 512 name the same owner, and some device reaches 512.
All inputs are finite; a program needn't handle non-finite values.
Results may differ from a plain program's by a relative error of at most 0.0075.
Values may be sent and summed in bfloat16 or wider, within the bound.
A program may use at most 128 MiB of HBM per device.

v0:
```python
import jax
import jax.numpy as jnp
from jax import lax
from jax.sharding import PartitionSpec as P

epsilon = 1e-06


def from_behind(block, axis, distance):
    devices = range(lax.axis_size(axis))
    route = [((i - distance) % len(devices), i) for i in devices]
    return lax.ppermute(block, axis, route)


def slot_numbers(owner_ids, group_size):
    onehot = (owner_ids[:, None] == jnp.arange(group_size, dtype=jnp.int32)[None, :]).astype(
        jnp.int32
    )
    earlier = jnp.cumsum(onehot, axis=0) - onehot
    return jnp.sum(earlier * onehot, axis=1)


def masked_products(requested, table_ids, tables):
    table_count = tables.shape[0]

    def add_table(table_index, running):
        chosen = jnp.where(
            (table_ids == table_index)[:, None], requested, jnp.zeros_like(requested)
        )
        return running + jnp.dot(chosen, tables[table_index], preferred_element_type=jnp.float32)

    total = lax.fori_loop(0, table_count, add_table, jnp.zeros(requested.shape, jnp.float32))
    return total.astype(jnp.bfloat16)


def squared_norm(field):
    return lax.psum(jnp.sum(field * field), ("blk", "grp"))


def projected(left_field, right_field):
    return lax.psum(jnp.sum(left_field * right_field), ("blk", "grp"))


def body(
    incident,
    mie_coef,
    owner_dev,
    near_row,
    table_id,
    tables,
    wave_out,
    wave_in,
    plane_angle,
    far_trans,
):
    source = incident[0]
    scatter_coef = mie_coef[0]
    owner_ids = owner_dev[0, :, 0]
    row_ids = near_row[0]
    table_ids = table_id[0]
    local_rows, coef_count = source.shape
    group_size = lax.axis_size("grp")
    blocks = lax.axis_size("blk")
    capacity = local_rows // 2
    per_row = owner_ids.shape[0] // local_rows
    cosine = jnp.cos(plane_angle[0].astype(jnp.float32))
    trans_rows = far_trans[0, 0]
    slot_ids = slot_numbers(owner_ids, group_size)
    my_block = lax.axis_index("blk")
    send_rows = jnp.zeros((group_size, capacity), jnp.int32).at[owner_ids, slot_ids].set(row_ids)
    wanted_rows = lax.all_to_all(send_rows, "grp", split_axis=0, concat_axis=0, tiled=True)

    def apply_operator(vector):
        coded_vec = vector.astype(jnp.bfloat16)
        picked = coded_vec[wanted_rows]
        answered = lax.all_to_all(picked, "grp", split_axis=0, concat_axis=0, tiled=True)
        near_terms = masked_products(answered[owner_ids, slot_ids], table_ids, tables)
        near_field = (
            near_terms.astype(jnp.float32).reshape(local_rows, per_row, coef_count).sum(axis=1)
        )
        outgoing = jnp.dot(coded_vec, wave_out, preferred_element_type=jnp.float32)
        own_wave = jnp.sum(cosine * outgoing, axis=0)

        def cycle_turn(turn_index, state_pair):
            moving, incoming = state_pair
            moving = from_behind(moving, "blk", 1)
            source_block = (my_block - turn_index) % blocks
            weights = lax.dynamic_index_in_dim(trans_rows, source_block, 0, keepdims=False)
            return (moving, incoming + weights * moving)

        moved_wave, incoming = lax.fori_loop(
            1, blocks, cycle_turn, (own_wave, jnp.zeros_like(own_wave))
        )
        spread = (cosine * incoming[None, :]).astype(jnp.bfloat16)
        far_field = jnp.dot(spread, wave_in, preferred_element_type=jnp.float32)
        return vector - scatter_coef * (near_field + far_field)

    initial_norm = jnp.sqrt(squared_norm(source) + epsilon)
    first_basis = source / initial_norm
    first_image = apply_operator(first_basis)
    diag_first = projected(first_basis, first_image)
    resid_first = first_image - diag_first * first_basis
    below_first = jnp.sqrt(squared_norm(resid_first) + epsilon)
    second_basis = resid_first / below_first
    second_image = apply_operator(second_basis)
    upper_second = projected(first_basis, second_image)
    partial_image = second_image - upper_second * first_basis
    diag_second = projected(second_basis, partial_image)
    resid_second = partial_image - diag_second * second_basis
    below_second = jnp.sqrt(squared_norm(resid_second) + epsilon)
    gram_aa = diag_first * diag_first + below_first * below_first
    gram_ab = diag_first * upper_second + below_first * diag_second
    gram_bb = upper_second * upper_second + diag_second * diag_second + below_second * below_second
    rhs_first = initial_norm * diag_first
    rhs_second = initial_norm * upper_second
    determinant = gram_aa * gram_bb - gram_ab * gram_ab
    coef_first = (gram_bb * rhs_first - gram_ab * rhs_second) / determinant
    coef_second = (gram_aa * rhs_second - gram_ab * rhs_first) / determinant
    solution = coef_first * first_basis + coef_second * second_basis
    residual = source - coef_first * first_image - coef_second * second_image
    zero_entry = jnp.zeros((), jnp.float32)
    hessenberg = jnp.stack(
        [
            jnp.stack([diag_first, upper_second]),
            jnp.stack([below_first, diag_second]),
            jnp.stack([zero_entry, below_second]),
        ]
    )
    return (solution[None], residual[None], hessenberg)


def solution(mesh):
    return jax.shard_map(
        body,
        mesh=mesh,
        in_specs=(
            P("blk", "grp", None),
            P("blk", "grp", None),
            P("blk", "grp", None),
            P("blk", "grp"),
            P("blk", "grp"),
            P(),
            P(),
            P(),
            P("blk", "grp", None),
            P("blk", "grp", None, None),
        ),
        out_specs=(P("blk", "grp", None), P("blk", "grp", None), P()),
        check_vma=False,
    )
```

profile of v0, /device:TPU:0, one launch (start us, length us, event | category | flops | bytes accessed | tf_op | source)
XLA Modules:
  0.0 947.3 jit_solution(4544695337967017977)
XLA Ops:
  1.5 4.6 reduce-window.6
  10.8 12.5 %scatter_custom_fusion = s32[8192]{0:T(1024)} fusion(s32[3072]{0:T(1024)S(1)} %broadcast_select_fusion, s32[3072]{0:T(1024)} %bitcast.137, s32[]{:T(128)} %constant.174.clone.1), kind=kCustom, calls=%fused_computation.77 | custom fusion | bytes 33280
  23.3 6.0 all-to-all-start
  29.3 68.1 %psum.42 = f32[]{:T(128)} all-reduce(f32[]{:T(128)} %fusion.26), channel_id=1, replica_groups=mesh['blk'=8,'grp'=16] {'blk','grp'}, use_global_device_ids=true, to_apply=%region_1.2 | all-reduce | flops 1 | bytes 8 | tf_op jit(solution)/shard_map/psum | solution.py:37
  98.5 32.9 %gather_fusion = bf16[8192,240]{1,0:T(8,128)(2,1)} fusion(bf16[1024,240]{1,0:T(8,128)(2,1)S(1)} %copy.21, s32[8192]{0:T(1024)S(1)} %broadcast_clamp_fusion), kind=kCustom, calls=%fused_computation | custom fusion | bytes 7897088 | tf_op jit(solution)/shard_map/gather | solution.py:75
  131.4 6.2 copy.22
  137.6 4.7 all-to-all-start.1
  142.3 8.3 fusion.14
  150.6 44.5 %all-to-all-done.1 = bf16[16,512,240]{1,2,0:T(8,128)(2,1)} async-done(((bf16[16,512,240]{1,2,0:T(8,128)(2,1)}), bf16[16,512,240]{1,2,0:T(8,128)(2,1)}, u32[]{:S(2)}, u32[]{:S(2)}) %all-to-all-start.1) | async-done | bytes 3932192 | tf_op jit(solution)/shard_map/all_to_all | solution.py:76
  195.1 6.3 copy.23
  201.3 52.4 %gather_fusion.1 = bf16[3072,240]{1,0:T(8,128)(2,1)} fusion(bf16[16,512,240]{2,1,0:T(8,128)(2,1)} %copy.23, s32[3072]{0:T(1024)S(1)} %bitcast.123), kind=kCustom, calls=%fused_computation.1 | custom fusion | bytes 2973696 | tf_op jit(solution)/shard_map/gather | solution.py:77
  253.7 27.2 %while.64 = (s32[]{:T(128)}, f32[3072,240]{0,1:T(8,128)S(1)}, s32[3072]{0:T(1024)S(1)}, bf16[3072,240]{1,0:T(8,128)(2,1)}, bf16[8,240,240]{2,1,0:T(8,128)(2,1)}, /*index=5*/s32[]{:T(128)}, s32[]{:T(128)}) while((s32[]{:T(128)}, f32[3072,240]{0,1:T(8,128)S(1)}, s32[3072]{0:T(1024)S(1)}, bf16[3072,240]{1,0:T(8,128)(2,1)}, ...), condition=%wide.region_7.8_spmd.clone, body=%wide.region_6.7_spmd.clone.sunk | while | flops 356109312 | bytes 7613019 | solution.py:32
  288.1 4.7 reduce_sum.104
  293.2 51.1 %while.65 = (s32[]{:T(128)}, f32[512]{0:T(512)S(1)}, f32[512]{0:T(512)S(1)}, s32[]{:T(128)}, f32[8,512]{1,0:T(8,128)}, /*index=5*/s32[]{:T(128)}, s32[]{:T(128)}, s32[]{:T(128)}, s32[]{:T(128)}) while((s32[]{:T(128)}, f32[512]{0:T(512)S(1)}, f32[512]{0:T(512)S(1)}, s32[]{:T(128)}, f32[8,512]{1,0:T(8,128)}, ...), condition=%wide.region_11.12_spmd.clone, body=%wide.region_10.11_spmd.clone.sunk | while | flops 1554 | bytes 24886 | solution.py:91
  295.8 4.7 collective-permute-done
  301.4 6.4 collective-permute-done
  308.7 6.4 collective-permute-done
  316.0 6.4 collective-permute-done
  323.3 6.4 collective-permute-done
  330.5 6.4 collective-permute-done
  337.8 6.4 collective-permute-done
  344.3 10.2 %multiply_reduce_fusion.4 = (f32[]{:T(128)}, f32[1024,240]{0,1:T(8,128)S(1)}) fusion(f32[]{:T(128)S(6)} %sqrt.9, f32[1,1024,240]{1,2,0:T(8,128)S(1)} %copy-done.2, f32[1024,240]{0,1:T(8,128)S(1)} %copy.25, bf16[512,240]{0,1:T(8,128)(2,1)S(1)} %copy-done, bf16[1,1024,512]{2,1,0:T(8,128)(2,1)} %param.26, f32[512]{0:T(512)S(1)} %get-tuple-element.458, ...), kind=kOutput, calls=%fused_computation.59 | convolution fusion | flops 254705664 | bytes 5228552 | tf_op jit(solution)/shard_map/dot_general | solution.py:95
  354.5 62.7 %psum.43 = f32[]{:T(128)} all-reduce(f32[]{:T(128)} %get-tuple-element.589), channel_id=1, replica_groups=mesh['blk'=8,'grp'=16] {'blk','grp'}, use_global_device_ids=true, to_apply=%region_13.14 | all-reduce | flops 1 | bytes 8 | tf_op jit(solution)/shard_map/psum | solution.py:41
  418.8 63.8 %psum.44 = f32[]{:T(128)} all-reduce(f32[]{:T(128)} %multiply_reduce_fusion.3), channel_id=1, replica_groups=mesh['blk'=8,'grp'=16] {'blk','grp'}, use_global_device_ids=true, to_apply=%region_15.16 | all-reduce | flops 1 | bytes 8 | tf_op jit(solution)/shard_map/psum | solution.py:37
  485.3 32.9 %gather_fusion.2 = bf16[8192,240]{1,0:T(8,128)(2,1)} fusion(bf16[1024,240]{1,0:T(8,128)(2,1)S(1)} %copy.26, s32[8192]{0:T(1024)S(1)} %broadcast_clamp_fusion), kind=kCustom, calls=%fused_computation.2 | custom fusion | bytes 7897088 | tf_op jit(solution)/shard_map/gather | solution.py:75
  518.2 6.2 copy.27
  524.4 4.5 all-to-all-start.2
  530.9 8.3 fusion.16
  539.2 42.5 %all-to-all-done.2 = bf16[16,512,240]{1,2,0:T(8,128)(2,1)} async-done(((bf16[16,512,240]{1,2,0:T(8,128)(2,1)}), bf16[16,512,240]{1,2,0:T(8,128)(2,1)}, u32[]{:S(2)}, u32[]{:S(2)}) %all-to-all-start.2) | async-done | bytes 3932192 | tf_op jit(solution)/shard_map/all_to_all | solution.py:76
  581.7 6.3 copy.28
  588.0 52.4 %gather_fusion.3 = bf16[3072,240]{1,0:T(8,128)(2,1)} fusion(bf16[16,512,240]{2,1,0:T(8,128)(2,1)} %copy.28, s32[3072]{0:T(1024)S(1)} %bitcast.124), kind=kCustom, calls=%fused_computation.3 | custom fusion | bytes 2973696 | tf_op jit(solution)/shard_map/gather | solution.py:77
  640.4 27.2 %while.66 = (s32[]{:T(128)}, f32[3072,240]{0,1:T(8,128)S(1)}, s32[3072]{0:T(1024)S(1)}, bf16[3072,240]{1,0:T(8,128)(2,1)}, bf16[8,240,240]{2,1,0:T(8,128)(2,1)}, /*index=5*/s32[]{:T(128)}, s32[]{:T(128)}) while((s32[]{:T(128)}, f32[3072,240]{0,1:T(8,128)S(1)}, s32[3072]{0:T(1024)S(1)}, bf16[3072,240]{1,0:T(8,128)(2,1)}, ...), condition=%wide.region_17.18_spmd.clone, body=%wide.region_16.17_spmd.clone.sunk | while | flops 356109312 | bytes 7613019 | solution.py:32
  647.2 3.4 convolution_add_fusion.7
  650.6 3.4 convolution_add_fusion.7
  657.4 3.4 convolution_add_fusion.7
  674.8 4.7 reduce_sum.108
  680.9 51.0 %while.67 = (s32[]{:T(128)}, f32[512]{0:T(512)S(1)}, f32[512]{0:T(512)S(1)}, s32[]{:T(128)}, f32[8,512]{1,0:T(8,128)}, /*index=5*/s32[]{:T(128)}, s32[]{:T(128)}, s32[]{:T(128)}, s32[]{:T(128)}) while((s32[]{:T(128)}, f32[512]{0:T(512)S(1)}, f32[512]{0:T(512)S(1)}, s32[]{:T(128)}, f32[8,512]{1,0:T(8,128)}, ...), condition=%wide.region_21.22_spmd.clone, body=%wide.region_20.21_spmd.clone.sunk | while | flops 1554 | bytes 24886 | solution.py:91
  683.4 4.7 collective-permute-done.1
  688.9 6.4 collective-permute-done.1
  696.2 6.4 collective-permute-done.1
  703.5 6.4 collective-permute-done.1
  710.8 6.4 collective-permute-done.1
  718.1 6.4 collective-permute-done.1
  725.4 6.4 collective-permute-done.1
  731.9 10.5 %multiply_reduce_fusion.2 = (f32[]{:T(128)}, f32[1024,240]{0,1:T(8,128)S(1)}) fusion(f32[]{:T(128)S(6)} %sqrt.9, f32[1,1024,240]{1,2,0:T(8,128)S(1)} %copy-done.3, f32[1024,240]{0,1:T(8,128)S(1)} %copy-done.4, f32[1024,240]{0,1:T(8,128)} %copy.30, bf16[512,240]{0,1:T(8,128)(2,1)S(1)} %copy-done, bf16[1,1024,512]{2,1,0:T(8,128)(2,1)} %param.26, ...), kind=kOutput, calls=%fused_computation.56 | convolution fusion | flops 254705664 | bytes 6211592 | tf_op jit(solution)/shard_map/dot_general | solution.py:95
  742.3 62.7 %psum.45 = f32[]{:T(128)} all-reduce(f32[]{:T(128)} %get-tuple-element.591), channel_id=1, replica_groups=mesh['blk'=8,'grp'=16] {'blk','grp'}, use_global_device_ids=true, to_apply=%region_23.24 | all-reduce | flops 1 | bytes 8 | tf_op jit(solution)/shard_map/psum | solution.py:41
  806.7 63.8 %psum.46 = f32[]{:T(128)} all-reduce(f32[]{:T(128)} %multiply_reduce_fusion.1), channel_id=1, replica_groups=mesh['blk'=8,'grp'=16] {'blk','grp'}, use_global_device_ids=true, to_apply=%region_25.26 | all-reduce | flops 1 | bytes 8 | tf_op jit(solution)/shard_map/psum | solution.py:41
  877.9 62.5 %psum.47 = f32[]{:T(128)} all-reduce(f32[]{:T(128)} %multiply_reduce_fusion), channel_id=1, replica_groups=mesh['blk'=8,'grp'=16] {'blk','grp'}, use_global_device_ids=true, to_apply=%region_27.28 | all-reduce | flops 1 | bytes 8 | tf_op jit(solution)/shard_map/psum | solution.py:37
  (141 shorter events, 93.7 us)
Async XLA Ops:
  0.6 343.7 %copy-start = (bf16[512,240]{0,1:T(8,128)(2,1)S(1)}, bf16[512,240]{0,1:T(8,128)(2,1)}, u32[]{:S(2)}) copy-start(bf16[512,240]{0,1:T(8,128)(2,1)} %param.25) | copy-start | bytes 737284
  0.6 9.3 copy-start.1
  23.3 75.1 %all-to-all-start = ((s32[16,1,512]{2,1,0:T(1,128)}), s32[16,1,512]{2,1,0:T(1,128)S(1)}, u32[]{:S(2)}, u32[]{:S(2)}) async-start(s32[16,1,512]{2,1,0:T(1,128)} %bitcast.9), calls=%async_computation | async-start | bytes 65536 | tf_op jit(solution)/shard_map/all_to_all | solution.py:71
  98.2 33.2 %copy-start.7 = (bf16[1024,240]{0,1:T(8,128)(2,1)}, bf16[1024,240]{0,1:T(8,128)(2,1)S(1)}, u32[]{:S(2)}) copy-start(bf16[1024,240]{0,1:T(8,128)(2,1)S(1)} %fusion.35) | copy-start | bytes 1474564
  137.6 57.4 %all-to-all-start.1 = ((bf16[16,512,240]{1,2,0:T(8,128)(2,1)}), bf16[16,512,240]{1,2,0:T(8,128)(2,1)}, u32[]{:S(2)}, u32[]{:S(2)}) async-start(bf16[16,512,240]{1,2,0:T(8,128)(2,1)} %copy.22), calls=%async_computation.1 | async-start | bytes 7864320 | tf_op jit(solution)/shard_map/all_to_all | solution.py:76
  201.3 52.4 %copy-start.8 = (s32[1,3072]{1,0:T(1,128)S(1)}, s32[1,3072]{1,0:T(1,128)}, u32[]{:S(2)}) copy-start(s32[1,3072]{1,0:T(1,128)} %param.22) | copy-start | bytes 36868
  292.9 51.4 %copy-start.2 = (f32[1,1024,240]{1,2,0:T(8,128)S(1)}, f32[1,1024,240]{1,2,0:T(8,128)}, u32[]{:S(2)}) copy-start(f32[1,1024,240]{1,2,0:T(8,128)} %param.18) | copy-start | bytes 2949124
  293.2 7.3 collective-permute-start
  300.5 7.3 collective-permute-start
  307.8 7.3 collective-permute-start
  315.1 7.3 collective-permute-start
  322.4 7.3 collective-permute-start
  329.7 7.3 collective-permute-start
  337.0 7.3 collective-permute-start
  354.5 130.6 %copy-start.5 = (f32[1024,240]{0,1:T(8,128)}, f32[1024,240]{0,1:T(8,128)S(1)}, u32[]{:S(2)}) copy-start(f32[1024,240]{0,1:T(8,128)S(1)} %get-tuple-element.590) | copy-start | bytes 2949124
  485.1 33.1 %copy-start.6 = (bf16[1024,240]{0,1:T(8,128)(2,1)}, bf16[1024,240]{0,1:T(8,128)(2,1)S(1)}, u32[]{:S(2)}) copy-start(bf16[1024,240]{0,1:T(8,128)(2,1)S(1)} %get-tuple-element.582) | copy-start | bytes 1474564
  524.4 57.3 %all-to-all-start.2 = ((bf16[16,512,240]{1,2,0:T(8,128)(2,1)}), bf16[16,512,240]{1,2,0:T(8,128)(2,1)}, u32[]{:S(2)}, u32[]{:S(2)}) async-start(bf16[16,512,240]{1,2,0:T(8,128)(2,1)} %copy.27), calls=%async_computation.2 | async-start | bytes 7864320 | tf_op jit(solution)/shard_map/all_to_all | solution.py:76
  679.6 52.3 %copy-start.3 = (f32[1,1024,240]{1,2,0:T(8,128)S(1)}, f32[1,1024,240]{1,2,0:T(8,128)}, u32[]{:S(2)}) copy-start(f32[1,1024,240]{1,2,0:T(8,128)} %param.18) | copy-start | bytes 2949124
  679.6 52.3 %copy-start.4 = (f32[1024,240]{0,1:T(8,128)S(1)}, f32[1024,240]{0,1:T(8,128)}, u32[]{:S(2)}) copy-start(f32[1024,240]{0,1:T(8,128)} %get-tuple-element.583) | copy-start | bytes 2949124
  680.9 7.2 collective-permute-start.1
  688.1 7.3 collective-permute-start.1
  695.4 7.3 collective-permute-start.1
  702.7 7.3 collective-permute-start.1
  710.0 7.3 collective-permute-start.1
  717.3 7.3 collective-permute-start.1
  724.6 7.3 collective-permute-start.1
where the time goes:
time: 961 us; the launch traced here: 947 us
  blocking collectives  384 us (40%)
  local copies, waits for them, and re-layouts  232 us (24%)
  waiting for transfers between devices  174 us (18%)
  matrix products  91 us (9%)
  other arithmetic  35.4 us (4%)
  starting transfers between devices  19.7 us (2%)
  between operations  10.6 us (1%)
    psum x3, blocking collectives, squared_norm(): return lax.psum(jnp.sum(field * field), ('blk', 'grp'))  194 us
    psum x3, blocking collectives, projected(): return lax.psum(jnp.sum(left_field * right_field), ('blk', 'grp'))  189 us
    gather x2, local copies, waits for them, and re-layouts, apply_operator(): answered[owner_ids, slot_ids]  105 us
    all_to_all x2, waiting for transfers between devices, apply_operator(): lax.all_to_all(picked, 'grp', split_axis=0, concat_axis=0, tiled=True)  87 us
    ppermute x14, waiting for transfers between devices, from_behind(): return lax.ppermute(block, axis, route)  86.6 us
    gather x4, local copies, waits for them, and re-layouts, apply_operator(): picked = coded_vec[wanted_rows]  78.2 us
    dot_general x16, matrix products, add_table(): jnp.dot(chosen, tables[table_index], preferred_element_type=jnp.float32)  53.8 us
    dot_general x2, matrix products, apply_operator(): far_field = jnp.dot(spread, wave_in, preferred_element_type=jnp.float32)  20.7 us
  transfers between devices with their start and end apart: 17, of which 16 were waited for; matrix products, arithmetic and copies ran while one was open for 3% of the time, Pallas kernels for 0%

commit v1 on v0

v1 whole, which is shorter than its diff:
```python
import functools

import jax
import jax.numpy as jnp
from jax import lax
from jax.experimental import pallas as pl
from jax.experimental.pallas import tpu as pltpu
from jax.sharding import PartitionSpec as P

MESH = pl.DeviceIdType.MESH
F32 = jnp.float32
BF16 = jnp.bfloat16

epsilon = 1e-06

ROWS = 1024
COEF = 240
WAVES = 512
TABLES = 8
PER_ROW = 3
GROUP = 16
BLOCKS = 8
CHUNKS = 8
CHUNK = ROWS // CHUNKS
TILE = 256
UNROLL = 32

Z_FIRST = (True, False, True, False, True, False, True, True)
GO_RIGHT = (True, False, False, True, True, False, False, True)


class Gather:
    def __init__(self, gbuf, send_sems, recv_sems):
        self.gbuf, self.send_sems, self.recv_sems = gbuf, send_sems, recv_sems
        g = lax.axis_index("grp")
        self.z, self.y, self.c = g // 8, (g // 2) % 4, g % 2
        self.me = g
        self.right = self.place(0, 1)
        self.left = self.place(0, 3)
        self.across = self.place(1, 0)
        self.partner = self.place(0, 0, 1)
        self.sent = []

    def place(self, dz, dy, dc=0):
        return ((self.z + dz) % 2) * 8 + ((self.y + dy) % 4) * 2 + (self.c + dc) % 2

    def copy(self, origin, chunk, device, slot):
        rows = pl.ds(pl.multiple_of(origin * ROWS + chunk * CHUNK, CHUNK), CHUNK)
        return pltpu.make_async_remote_copy(
            src_ref=self.gbuf.at[rows],
            dst_ref=self.gbuf.at[rows],
            send_sem=self.send_sems.at[slot],
            recv_sem=self.recv_sems.at[origin, chunk],
            device_id={"grp": device},
            device_id_type=MESH,
        )

    def send(self, origin, chunk, *devices):
        for device in devices:
            copy = self.copy(origin, chunk, device, len(self.sent))
            copy.start()
            self.sent.append(copy)

    def wait(self, origin, chunk):
        self.copy(origin, chunk, self.partner, 0).wait_recv()

    def start(self):
        for k in range(CHUNKS):
            self.send(self.me, k, self.right, self.left, self.across, self.partner)

    def level_one(self):
        for k in range(CHUNKS):
            extra = () if Z_FIRST[k] else (self.across,)
            origin = self.place(0, 3)
            self.wait(origin, k)
            self.send(origin, k, *((self.right,) if GO_RIGHT[k] else ()), *extra, self.partner)
            origin = self.place(0, 1)
            self.wait(origin, k)
            self.send(origin, k, *(() if GO_RIGHT[k] else (self.left,)), *extra, self.partner)
            origin = self.place(1, 0)
            self.wait(origin, k)
            self.send(origin, k, *((self.right, self.left) if Z_FIRST[k] else ()), self.partner)

    def level_two(self):
        for k in range(CHUNKS):
            origin = self.place(0, 2)
            self.wait(origin, k)
            self.send(origin, k, *(() if Z_FIRST[k] else (self.across,)), self.partner)
            origin = self.place(1, 3)
            self.wait(origin, k)
            self.send(origin, k, *((self.right,) if Z_FIRST[k] and GO_RIGHT[k] else ()), self.partner)
            origin = self.place(1, 1)
            self.wait(origin, k)
            self.send(origin, k, *((self.left,) if Z_FIRST[k] and not GO_RIGHT[k] else ()), self.partner)

    def level_three(self):
        for k in range(CHUNKS):
            origin = self.place(1, 2)
            self.wait(origin, k)
            self.send(origin, k, self.partner)

    def finish(self):
        for dz in range(2):
            for dy in (0, 1, 3, 2):
                for k in range(CHUNKS):
                    self.wait(self.place(dz, dy, 1), k)
        for copy in self.sent:
            copy.wait_send()
        self.sent = []


SENDS = CHUNKS * 4 + sum(
    (3 if z else 5) + 1 + (2 if z else 0) + 1 + 3 + (0 if z else 1) + (1 if z else 0) for z in Z_FIRST
)


def shared(buf, send_sems, recv_sems, axis, size, slot):
    copies = []
    for step in range(1, size):
        copy = pltpu.make_async_remote_copy(
            src_ref=buf.at[slot],
            dst_ref=buf.at[slot],
            send_sem=send_sems.at[step - 1],
            recv_sem=recv_sems.at[slot],
            device_id={axis: (slot + step) % size},
            device_id_type=MESH,
        )
        copy.start()
        copies.append(copy)
    return copies


def collect(copies, buf, send_sems, recv_sems, axis, size, slot):
    for step in range(1, size):
        source = (slot + step) % size
        pltpu.make_async_remote_copy(
            src_ref=buf.at[source],
            dst_ref=buf.at[source],
            send_sem=send_sems.at[step - 1],
            recv_sem=recv_sems.at[source],
            device_id={axis: source},
            device_id_type=MESH,
        ).wait_recv()
    for copy in copies:
        copy.wait_send()


def row_of(*values):
    lane = lax.broadcasted_iota(jnp.int32, (1, 128), 1)
    row = jnp.zeros((1, 128), F32)
    for place, value in enumerate(values):
        row = jnp.where(lane == place, value, row)
    return row


def column(rows, place):
    lane = lax.broadcasted_iota(jnp.int32, rows.shape, 1)
    return jnp.sum(jnp.where(lane == place, rows, 0.0), axis=1, keepdims=True)


def total(value):
    return jnp.sum(jnp.sum(value, axis=0, keepdims=True), axis=1, keepdims=True)


def spread_stats(rows):
    squares, inner, left, slope = (column(rows, place) for place in range(4))
    squares_all = jnp.sum(squares, axis=0, keepdims=True)
    inner_all = jnp.sum(inner, axis=0, keepdims=True)
    slope_all = inner_all / jnp.maximum(squares_all, 1e-30)
    gap = slope - slope_all
    left_all = jnp.sum(left + gap * gap * squares, axis=0, keepdims=True)
    return squares_all, inner_all, left_all, slope_all


def kernel(
    source_rows,
    table_ids,
    u_ref,
    mie_ref,
    tables_ref,
    wave_out_ref,
    wave_in_ref,
    angle_ref,
    trans_ref,
    sol_ref,
    res_ref,
    hess_ref,
    gbuf,
    picked,
    ids,
    padded,
    cosine,
    base,
    w1_ref,
    v2_ref,
    w2_ref,
    wbuf,
    stats_a,
    stats_b,
    ag_send,
    ag_recv,
    w_send,
    w_recv,
    a_send,
    a_recv,
    b_send,
    b_recv,
):
    g = lax.axis_index("grp")
    b = lax.axis_index("blk")
    barrier = pltpu.get_barrier_semaphore()
    for step in range(1, GROUP):
        pl.semaphore_signal(barrier, inc=1, device_id={"grp": (g + step) % GROUP}, device_id_type=MESH)
    for step in range(1, BLOCKS):
        pl.semaphore_signal(barrier, inc=1, device_id={"blk": (b + step) % BLOCKS}, device_id_type=MESH)
    pl.semaphore_wait(barrier, GROUP + BLOCKS - 2)

    gather = Gather(gbuf, ag_send, ag_recv)

    def exchange(turn, row, combine):
        stats_a[turn, pl.ds(g, 1)] = row.reshape(1, 1, 128)
        near_buf = stats_a.at[turn]
        copies = shared(near_buf, a_send, a_recv, "grp", GROUP, g)
        collect(copies, near_buf, a_send, a_recv, "grp", GROUP, g)
        row = combine(stats_a[turn].reshape(GROUP, 128))
        stats_b[turn, pl.ds(b, 1)] = row.reshape(1, 1, 128)
        far_buf = stats_b.at[turn]
        copies = shared(far_buf, b_send, b_recv, "blk", BLOCKS, b)
        collect(copies, far_buf, b_send, b_recv, "blk", BLOCKS, b)
        return stats_b[turn].reshape(BLOCKS, 128)

    def prepare():
        padded[...] = jnp.zeros_like(padded)
        for t in range(TABLES):
            padded[t, 0:COEF, :] = tables_ref[t]
        for k in range(PER_ROW):

            @pl.loop(0, ROWS // UNROLL)
            def _(turn):
                for step in range(UNROLL):
                    row = turn * UNROLL + step
                    value = table_ids[row * PER_ROW + k]
                    ids[pl.ds(k * ROWS + row, 1), :] = jnp.full((1, 128), value, jnp.int32).astype(F32)

        @pl.loop(0, ROWS // TILE)
        def _(tile):
            rows = pl.ds(pl.multiple_of(tile * TILE, TILE), TILE)
            cosine[rows, :] = jnp.cos(angle_ref[rows, :].astype(F32))

    def operate(vec_ref, out_ref, first):
        @pl.loop(0, ROWS // TILE)
        def _(tile):
            start = pl.multiple_of(tile * TILE, TILE)
            coded = vec_ref[pl.ds(start, TILE), :].astype(BF16)
            wide = jnp.concatenate([coded, jnp.zeros((TILE, 256 - COEF), BF16)], axis=1)
            gbuf[pl.ds(pl.multiple_of(g * ROWS + start, TILE), TILE)] = wide.reshape(TILE, 2, 128)

        gather.start()
        if first:
            prepare()

        def far_out(tile, wave):
            rows = pl.ds(pl.multiple_of(tile * TILE, TILE), TILE)
            coded = vec_ref[rows, :].astype(BF16)
            outgoing = jnp.dot(coded, wave_out_ref[...], preferred_element_type=F32)
            return wave + jnp.sum(cosine[rows, :] * outgoing, axis=0, keepdims=True)

        wave = lax.fori_loop(0, ROWS // TILE, far_out, jnp.zeros((1, WAVES), F32))
        wbuf[pl.ds(b, 1)] = wave.reshape(1, 1, WAVES)
        wave_copies = shared(wbuf, w_send, w_recv, "blk", BLOCKS, b)
        gather.level_one()
        collect(wave_copies, wbuf, w_send, w_recv, "blk", BLOCKS, b)
        incoming = jnp.zeros((1, WAVES), F32)
        for c in range(BLOCKS):
            term = trans_ref[c : c + 1, :] * wbuf[c]
            incoming = incoming + jnp.where(b == c, jnp.zeros_like(term), term)

        @pl.loop(0, ROWS // TILE)
        def _(tile):
            rows = pl.ds(pl.multiple_of(tile * TILE, TILE), TILE)
            spread = (cosine[rows, :] * incoming).astype(BF16)
            base[rows, :] = jnp.dot(spread, wave_in_ref[...], preferred_element_type=F32)

        gather.level_two()
        gather.level_three()
        gather.finish()

        for k in range(PER_ROW):

            @pl.loop(0, ROWS // UNROLL)
            def _(turn):
                first_row = turn * UNROLL
                places = [source_rows[(first_row + step) * PER_ROW + k] for step in range(UNROLL)]
                values = [gbuf[place].astype(F32) for place in places]
                for step, value in enumerate(values):
                    picked[pl.ds((k * ROWS + first_row + step) * 2, 2), :] = value

        @pl.loop(0, ROWS // TILE)
        def _(tile):
            start = pl.multiple_of(tile * TILE, TILE)
            rows = pl.ds(start, TILE)
            near = jnp.zeros((TILE, COEF), F32)
            for k in range(PER_ROW):
                low = picked[pl.ds(2 * (k * ROWS + start), TILE, 2), :]
                high = picked[pl.ds(2 * (k * ROWS + start) + 1, TILE, 2), :]
                wanted = jnp.concatenate([low, high], axis=1).astype(BF16)
                table = ids[pl.ds(k * ROWS + start, TILE), :]
                table = jnp.concatenate([table, table], axis=1).astype(BF16)
                term = jnp.zeros((TILE, COEF), F32)
                for t in range(TABLES):
                    chosen = jnp.where(table == jnp.asarray(t, BF16), wanted, jnp.zeros_like(wanted))
                    term = term + jnp.dot(chosen, padded[t], preferred_element_type=F32)
                near = near + term.astype(BF16).astype(F32)
            out_ref[rows, :] = vec_ref[rows, :] - mie_ref[rows, :] * (near + base[rows, :])

    def tiles(step, count):
        return lax.fori_loop(0, ROWS // TILE, step, (jnp.zeros((1, 1), F32),) * count)

    def tile_rows(tile):
        return pl.ds(pl.multiple_of(tile * TILE, TILE), TILE)

    operate(u_ref, w1_ref, True)

    def first_sums(tile, sums):
        rows = tile_rows(tile)
        u, w = u_ref[rows, :], w1_ref[rows, :]
        return sums[0] + total(u * u), sums[1] + total(u * w)

    squares, inner = tiles(first_sums, 2)
    slope = inner / jnp.maximum(squares, 1e-30)

    def left_sum(tile, sums):
        rows = tile_rows(tile)
        rest = w1_ref[rows, :] - slope * u_ref[rows, :]
        return (sums[0] + total(rest * rest),)

    (left,) = tiles(left_sum, 1)
    parts = exchange(0, row_of(squares, inner, left, slope), lambda rows: row_of(*spread_stats(rows)))
    squares, inner, left, slope = spread_stats(parts)
    beta_squared = squares + epsilon
    beta = jnp.sqrt(beta_squared)
    h11 = inner / beta_squared
    gap = slope - h11
    h21 = jnp.sqrt((left + gap * gap * squares) / beta_squared + epsilon)
    scale = 1.0 / (beta * h21)

    @pl.loop(0, ROWS // TILE)
    def _(tile):
        rows = tile_rows(tile)
        v2_ref[rows, :] = (w1_ref[rows, :] - h11 * u_ref[rows, :]) * scale

    operate(v2_ref, w2_ref, False)

    def second_sums(tile, sums):
        rows = tile_rows(tile)
        u, v, w = u_ref[rows, :], v2_ref[rows, :], w2_ref[rows, :]
        pairs = (u * w, v * w, w * w, u * v, v * v)
        return tuple(have + total(pair) for have, pair in zip(sums, pairs))

    sums = tiles(second_sums, 5)
    parts = exchange(1, row_of(*sums), lambda rows: jnp.sum(rows, axis=0, keepdims=True))
    uw, vw, ww, uv, vv = (column(jnp.sum(parts, axis=0, keepdims=True), place) for place in range(5))
    h12 = uw / beta
    h22 = vw
    left = ww + h12 * h12 * (squares / beta_squared - 2.0) + h22 * h22 * (vv - 2.0) + 2.0 * h12 * h22 * (uv / beta)
    h32 = jnp.sqrt(jnp.maximum(left, 0.0) + epsilon)
    gram_aa = h11 * h11 + h21 * h21
    gram_ab = h11 * h12 + h21 * h22
    gram_bb = h12 * h12 + h22 * h22 + h32 * h32
    rhs_first = beta * h11
    rhs_second = beta * h12
    determinant = gram_aa * gram_bb - gram_ab * gram_ab
    y1 = (gram_bb * rhs_first - gram_ab * rhs_second) / determinant
    y2 = (gram_aa * rhs_second - gram_ab * rhs_first) / determinant
    y1_scaled = y1 / beta

    @pl.loop(0, ROWS // TILE)
    def _(tile):
        rows = tile_rows(tile)
        u = u_ref[rows, :]
        sol_ref[rows, :] = y1_scaled * u + y2 * v2_ref[rows, :]
        res_ref[rows, :] = u - y1_scaled * w1_ref[rows, :] - y2 * w2_ref[rows, :]

    at_row = lax.broadcasted_iota(jnp.int32, (3, 2), 0)
    at_col = lax.broadcasted_iota(jnp.int32, (3, 2), 1)
    left_col = jnp.where(at_row == 0, h11, jnp.where(at_row == 1, h21, jnp.zeros((3, 2), F32)))
    right_col = jnp.where(at_row == 0, h12, jnp.where(at_row == 1, h22, h32))
    hess_ref[...] = jnp.where(at_col == 0, left_col, right_col)


def body(incident, mie_coef, owner_dev, near_row, table_id, tables, wave_out, wave_in, plane_angle, far_trans):
    source_rows = owner_dev[0, :, 0] * ROWS + near_row[0]
    vmem = pl.BlockSpec(memory_space=pltpu.VMEM)
    smem = pl.BlockSpec(memory_space=pltpu.SMEM)
    dma = pltpu.SemaphoreType.DMA
    sol, res, hess = pl.pallas_call(
        kernel,
        out_shape=(
            jax.ShapeDtypeStruct((ROWS, COEF), F32),
            jax.ShapeDtypeStruct((ROWS, COEF), F32),
            jax.ShapeDtypeStruct((3, 2), F32),
        ),
        in_specs=[smem, smem] + [vmem] * 7,
        out_specs=(vmem, vmem, vmem),
        scratch_shapes=[
            pltpu.VMEM((GROUP * ROWS, 2, 128), BF16),
            pltpu.VMEM((PER_ROW * ROWS * 2, 128), F32),
            pltpu.VMEM((PER_ROW * ROWS, 128), F32),
            pltpu.VMEM((TABLES, 256, COEF), BF16),
            pltpu.VMEM((ROWS, WAVES), F32),
            pltpu.VMEM((ROWS, COEF), F32),
            pltpu.VMEM((ROWS, COEF), F32),
            pltpu.VMEM((ROWS, COEF), F32),
            pltpu.VMEM((ROWS, COEF), F32),
            pltpu.VMEM((BLOCKS, 1, WAVES), F32),
            pltpu.VMEM((2, GROUP, 1, 128), F32),
            pltpu.VMEM((2, BLOCKS, 1, 128), F32),
            dma((SENDS,)),
            dma((GROUP, CHUNKS)),
            dma((BLOCKS - 1,)),
            dma((BLOCKS,)),
            dma((GROUP - 1,)),
            dma((GROUP,)),
            dma((BLOCKS - 1,)),
            dma((BLOCKS,)),
        ],
        compiler_params=pltpu.CompilerParams(
            collective_id=0, has_side_effects=True, vmem_limit_bytes=62 * 2**20
        ),
    )(
        source_rows,
        table_id[0],
        incident[0],
        mie_coef[0],
        tables,
        wave_out,
        wave_in,
        plane_angle[0],
        far_trans[0, 0],
    )
    return sol[None], res[None], hess


def solution(mesh):
    return jax.shard_map(
        body,
        mesh=mesh,
        in_specs=(
            P("blk", "grp", None),
            P("blk", "grp", None),
            P("blk", "grp", None),
            P("blk", "grp"),
            P("blk", "grp"),
            P(),
            P(),
            P(),
            P("blk", "grp", None),
            P("blk", "grp", None, None),
        ),
        out_specs=(P("blk", "grp", None), P("blk", "grp", None), P()),
        check_vma=False,
    )
```

time: 961 us -> 126 us (0.13); the launches traced: 947 us -> 126 us
  blocking collectives: 384 us -> 0 us
  local copies, waits for them, and re-layouts: 232 us -> 10.2 us
  waiting for transfers between devices: 174 us -> 0 us
  Pallas kernels: 0 us -> 114 us
  matrix products: 91 us -> 0 us
  other arithmetic: 35.4 us -> 1.33 us
  starting transfers between devices: 19.7 us -> 0 us
  between operations: 10.6 us -> 0.67 us
    psum x6 -> x0, blocking collectives: 384 us -> none  [the longest x3 194 us: squared_norm(): return lax.psum(jnp.sum(field * field), ('blk', 'grp'))]
    gather x6 -> x0, local copies, waits for them, and re-layouts: 183 us -> none  [the longest x2 105 us: apply_operator(): answered[owner_ids, slot_ids]]
    pallas_call x0 -> x1, Pallas kernels: none -> 114 us  [body(): pl.pallas_call(kernel, out_shape=(jax.ShapeDtypeStruct((ROWS, COEF), F32)...]
    dot_general x20 -> x0, matrix products: 91 us -> none  [the longest x16 53.8 us: add_table(): jnp.dot(chosen, tables[table_index], preferred_element_type=jnp.float32)]
    all_to_all x3 -> x0, waiting for transfers between devices: 87 us -> none  [the longest x2 87 us: apply_operator(): lax.all_to_all(picked, 'grp', split_axis=0, concat_axis=0, tiled=True)]
    ppermute x14 -> x0, waiting for transfers between devices: 86.6 us -> none  [from_behind(): return lax.ppermute(block, axis, route)]
    reduce_sum x7 -> x0, other arithmetic: 16.5 us -> none  [the longest x2 9.49 us: apply_operator(): near_terms.astype(jnp.float32).reshape(local_rows, per_row, coef_count)]
    all_to_all x3 -> x0, starting transfers between devices: 15.2 us -> none  [the longest x2 9.19 us: apply_operator(): lax.all_to_all(picked, 'grp', split_axis=0, concat_axis=0, tiled=True)]
  transfers between devices with their start and end apart: 17 -> 0, of which waited for: 16 -> 0; matrix products, arithmetic and copies ran while one was open for 3% -> 0% of each run, Pallas kernels for 0% -> 0%
where the time goes in v1:
time: 126 us
  Pallas kernels  114 us (90%)
  local copies, waits for them, and re-layouts  10.2 us (8%)
  other arithmetic  1.33 us (1%)
    pallas_call x1, Pallas kernels, body(): pl.pallas_call(kernel, out_shape=(jax.ShapeDtypeStruct((ROWS, COEF), F32)...  114 us
    unnamed x14, local copies, waits for them, and re-layouts  10.2 us

profile of v1, /device:TPU:0, one launch (start us, length us, event | category | flops | bytes accessed | tf_op | source)
XLA Modules:
  0.0 126.0 jit_solution(12823359875261702767)
XLA Ops:
  0.6 0.0 copy-start.2
  0.6 0.7 broadcast_multiply_fusion
  1.4 0.0 copy-done.2
  1.4 0.6 add.3.source_rows
  2.0 1.8 %copy.15.wave_in_ref = bf16[512,240]{1,0:T(8,128)(2,1)} copy(bf16[512,240]{0,1:T(8,128)(2,1)} %param.17) | data formatting | bytes 491520 | tf_op args[7]
  3.8 0.0 copy-start.1
  3.8 2.6 %copy.13 = f32[1,1024,240]{2,1,0:T(8,128)} copy(f32[1,1024,240]{1,2,0:T(8,128)} %param.10) | data formatting | bytes 1966080 | tf_op args[0]
  6.4 0.0 copy-done.1
  6.4 1.3 %copy.14 = f32[1,1024,240]{2,1,0:T(8,128)} copy(f32[1,1024,240]{1,2,0:T(8,128)S(1)} %copy-done.1) | data formatting | bytes 1966080 | tf_op args[1]
  7.7 113.7 %shard_map.121 = (f32[1024,240]{1,0:T(8,128)}, f32[1024,240]{1,0:T(8,128)}, f32[3,2]{1,0:T(4,128)}) custom-call(s32[3072]{0:T(1024)} %add.3.source_rows, s32[3072]{0:T(1024)} %bitcast.16, f32[1024,240]{1,0:T(8,128)} %bitcast.9, f32[1024,240]{1,0:T(8,128)} %bitcast.10, bf16[8,240,240]{2,1,0:T(8,128)(2,1)} %tables_ref.1, bf16[240,512]{1,0:T(8,128)(2,1)} %wave_out_ref.1, ...), custom_call_target="tpu_custom_call" | custom-call | tf_op jit(solution)/shard_map/pallas_call | solution.py:396
  121.5 0.0 copy-start
  121.5 2.6 %copy.16 = f32[1,1024,240]{1,2,0:T(8,128)} copy(f32[1,1024,240]{2,1,0:T(8,128)} %bitcast.12) | data formatting | bytes 1966080
  124.1 0.0 copy-done
  124.1 0.0 copy-start.3
  124.1 1.3 %copy.17 = f32[1,1024,240]{1,2,0:T(8,128)} copy(f32[1,1024,240]{2,1,0:T(8,128)S(1)} %bitcast.11) | data formatting | bytes 1966080
  125.3 0.0 copy-done.3
  125.3 0.6 copy.18
Async XLA Ops:
  0.6 0.7 copy-start.2
  3.8 2.6 %copy-start.1 = (f32[1,1024,240]{1,2,0:T(8,128)S(1)}, f32[1,1024,240]{1,2,0:T(8,128)}, u32[]{:S(2)}) copy-start(f32[1,1024,240]{1,2,0:T(8,128)} %param.11) | copy-start | bytes 2949124
  121.5 2.6 %copy-start = (f32[1024,240]{1,0:T(8,128)S(1)}, f32[1024,240]{1,0:T(8,128)}, u32[]{:S(2)}) copy-start(f32[1024,240]{1,0:T(8,128)} %get-tuple-element.7) | copy-start | bytes 2949124
  124.1 1.3 %copy-start.3 = (f32[3,2]{1,0:T(4,128)S(1)}, f32[3,2]{1,0:T(4,128)}, u32[]{:S(2)}) copy-start(f32[3,2]{1,0:T(4,128)} %get-tuple-element.11) | copy-start | bytes 76

commit v2 on v1

v2 whole, which is shorter than its diff:
```python
import functools

import jax
import jax.numpy as jnp
from jax import lax
from jax.experimental import pallas as pl
from jax.experimental.pallas import tpu as pltpu
from jax.sharding import PartitionSpec as P

MESH = pl.DeviceIdType.MESH
F32 = jnp.float32
BF16 = jnp.bfloat16

epsilon = 1e-06

ROWS = 1024
COEF = 240
WAVES = 512
TABLES = 8
PER_ROW = 3
GROUP = 16
BLOCKS = 8
CHUNKS = 16
CHUNK = ROWS // CHUNKS
TILE = 256
TILES = ROWS // TILE
UNROLL = 32

Z_FIRST = (True, False, True, False, True, False, True, False, True, False, True, False, True, False, True, True)
GO_RIGHT = (True, True, False, False, True, True, False, False, True, True, False, False, True, False, False, True)


class Gather:
    def __init__(self, gbuf, send_sems, recv_sems):
        self.gbuf, self.send_sems, self.recv_sems = gbuf, send_sems, recv_sems
        g = lax.axis_index("grp")
        self.z, self.y, self.c = g // 8, (g // 2) % 4, g % 2
        self.me = g
        self.right = self.place(0, 1)
        self.left = self.place(0, 3)
        self.across = self.place(1, 0)
        self.partner = self.place(0, 0, 1)
        self.sent = []

    def place(self, dz, dy, dc=0):
        return ((self.z + dz) % 2) * 8 + ((self.y + dy) % 4) * 2 + (self.c + dc) % 2

    def copy(self, origin, chunk, device, slot):
        rows = pl.ds(pl.multiple_of(origin * ROWS + chunk * CHUNK, CHUNK), CHUNK)
        return pltpu.make_async_remote_copy(
            src_ref=self.gbuf.at[rows],
            dst_ref=self.gbuf.at[rows],
            send_sem=self.send_sems.at[slot],
            recv_sem=self.recv_sems.at[origin, chunk],
            device_id={"grp": device},
            device_id_type=MESH,
        )

    def send(self, origin, chunk, *devices):
        for device in devices:
            copy = self.copy(origin, chunk, device, len(self.sent))
            copy.start()
            self.sent.append(copy)

    def wait(self, origin, chunk):
        self.copy(origin, chunk, self.partner, 0).wait_recv()

    def store(self, tile, coded):
        start = pl.multiple_of(self.me * ROWS + tile * TILE, TILE)
        self.gbuf[pl.ds(start, TILE)] = coded.reshape(TILE, 2, 128)

    def start(self, tile):
        for k in range(tile * TILE // CHUNK, (tile + 1) * TILE // CHUNK):
            self.send(self.me, k, self.right, self.left, self.across, self.partner)

    def level_one(self):
        for k in range(CHUNKS):
            extra = () if Z_FIRST[k] else (self.across,)
            origin = self.place(0, 3)
            self.wait(origin, k)
            self.send(origin, k, *((self.right,) if GO_RIGHT[k] else ()), *extra, self.partner)
            origin = self.place(0, 1)
            self.wait(origin, k)
            self.send(origin, k, *(() if GO_RIGHT[k] else (self.left,)), *extra, self.partner)
            origin = self.place(1, 0)
            self.wait(origin, k)
            self.send(origin, k, *((self.right, self.left) if Z_FIRST[k] else ()), self.partner)

    def level_two(self):
        for k in range(CHUNKS):
            origin = self.place(0, 2)
            self.wait(origin, k)
            self.send(origin, k, *(() if Z_FIRST[k] else (self.across,)), self.partner)
            origin = self.place(1, 3)
            self.wait(origin, k)
            self.send(origin, k, *((self.right,) if Z_FIRST[k] and GO_RIGHT[k] else ()), self.partner)
            origin = self.place(1, 1)
            self.wait(origin, k)
            self.send(origin, k, *((self.left,) if Z_FIRST[k] and not GO_RIGHT[k] else ()), self.partner)

    def level_three(self):
        for k in range(CHUNKS):
            origin = self.place(1, 2)
            self.wait(origin, k)
            self.send(origin, k, self.partner)

    def finish(self):
        for dz in range(2):
            for dy in (0, 1, 3, 2):
                for k in range(CHUNKS):
                    self.wait(self.place(dz, dy, 1), k)

    def drain(self):
        for copy in self.sent:
            copy.wait_send()


SENDS = CHUNKS * 15


class Share:
    def __init__(self, buf, send_sems, recv_sems, axis, size):
        self.buf, self.send_sems, self.recv_sems, self.axis, self.size = buf, send_sems, recv_sems, axis, size
        self.slot = lax.axis_index(axis)

    def copy(self, source, target, step):
        return pltpu.make_async_remote_copy(
            src_ref=self.buf.at[source],
            dst_ref=self.buf.at[source],
            send_sem=self.send_sems.at[step - 1],
            recv_sem=self.recv_sems.at[source],
            device_id={self.axis: target},
            device_id_type=MESH,
        )

    def start(self, row):
        self.buf[pl.ds(self.slot, 1)] = row.reshape(1, 1, row.shape[1])
        for step in range(1, self.size):
            self.copy(self.slot, (self.slot + step) % self.size, step).start()

    def finish(self):
        for step in range(1, self.size):
            other = (self.slot + step) % self.size
            self.copy(other, other, step).wait_recv()
        for step in range(1, self.size):
            self.copy(self.slot, (self.slot + step) % self.size, step).wait_send()
        return self.buf[...].reshape(self.size, self.buf.shape[2])


def row_of(*values):
    lane = lax.broadcasted_iota(jnp.int32, (1, 128), 1)
    row = jnp.zeros((1, 128), F32)
    for place, value in enumerate(values):
        row = jnp.where(lane == place, value, row)
    return row


def column(rows, place):
    lane = lax.broadcasted_iota(jnp.int32, rows.shape, 1)
    return jnp.sum(jnp.where(lane == place, rows, 0.0), axis=1, keepdims=True)


def total(value):
    return jnp.sum(jnp.sum(value, axis=0, keepdims=True), axis=1, keepdims=True)


def spread_stats(rows):
    squares, inner, left, slope = (column(rows, place) for place in range(4))
    squares_all = jnp.sum(squares, axis=0, keepdims=True)
    inner_all = jnp.sum(inner, axis=0, keepdims=True)
    slope_all = inner_all / jnp.maximum(squares_all, 1e-30)
    gap = slope - slope_all
    left_all = jnp.sum(left + gap * gap * squares, axis=0, keepdims=True)
    return squares_all, inner_all, left_all, slope_all


def rows_of(tile):
    return pl.ds(pl.multiple_of(tile * TILE, TILE), TILE)


def turned(tall):
    return jnp.concatenate([tall, jnp.zeros((256 - COEF, TILE), tall.dtype)], axis=0).T


def kernel(
    owners,
    near_rows,
    table_ids,
    u_ref,
    mie_hbm,
    tables_hbm,
    wave_out_hbm,
    wave_in_hbm,
    angle_hbm,
    trans_ref,
    b1_hbm,
    q_hbm,
    scal_ref,
    hess_ref,
    gbuf_a,
    gbuf_b,
    places,
    picked,
    ids,
    padded,
    cosine,
    base,
    coded,
    mie,
    mie_tall,
    tables,
    wave_out,
    wave_in,
    wave_in_tall,
    angle,
    b1_tall,
    q_tall,
    wbuf_a,
    wbuf_b,
    stats_a,
    stats_b,
    stats_c,
    stats_d,
    in_sems,
    out_sems,
    aga_send,
    aga_recv,
    agb_send,
    agb_recv,
    wa_send,
    wa_recv,
    wb_send,
    wb_recv,
    a_send,
    a_recv,
    b_send,
    b_recv,
    c_send,
    c_recv,
    d_send,
    d_recv,
):
    g = lax.axis_index("grp")
    b = lax.axis_index("blk")
    barrier = pltpu.get_barrier_semaphore()
    for step in range(1, GROUP):
        pl.semaphore_signal(barrier, inc=1, device_id={"grp": (g + step) % GROUP}, device_id_type=MESH)
    for step in range(1, BLOCKS):
        pl.semaphore_signal(barrier, inc=1, device_id={"blk": (b + step) % BLOCKS}, device_id_type=MESH)

    loads = [
        pltpu.make_async_copy(source, target, in_sems.at[place])
        for place, (source, target) in enumerate(
            (
                (angle_hbm, angle),
                (wave_out_hbm, wave_out),
                (wave_in_hbm, wave_in_tall),
                (mie_hbm, mie_tall),
                (tables_hbm, tables),
            )
        )
    ]
    for load in loads:
        load.start()

    first = Gather(gbuf_a, aga_send, aga_recv)
    second = Gather(gbuf_b, agb_send, agb_recv)
    waves_first = Share(wbuf_a, wa_send, wa_recv, "blk", BLOCKS)
    waves_second = Share(wbuf_b, wb_send, wb_recv, "blk", BLOCKS)
    share_a = Share(stats_a, a_send, a_recv, "grp", GROUP)
    share_b = Share(stats_b, b_send, b_recv, "blk", BLOCKS)
    share_c = Share(stats_c, c_send, c_recv, "grp", GROUP)
    share_d = Share(stats_d, d_send, d_recv, "blk", BLOCKS)

    for tile in range(TILES):
        block = turned(u_ref[:, tile * TILE : (tile + 1) * TILE]).astype(BF16)
        coded[rows_of(tile), :] = block
        first.store(tile, block)
        if tile == 0:
            pl.semaphore_wait(barrier, GROUP + BLOCKS - 2)
        first.start(tile)

    def tall_sums(step, count):
        sums = (jnp.zeros((1, 1), F32),) * count
        for tile in range(TILES):
            sums = step(slice(tile * TILE, (tile + 1) * TILE), sums)
        return sums

    def own_wave():
        def step(tile, wave):
            rows = rows_of(tile)
            outgoing = jnp.dot(coded[rows, 0:COEF], wave_out[...], preferred_element_type=F32)
            return wave + jnp.sum(cosine[rows, :] * outgoing, axis=0, keepdims=True)

        return lax.fori_loop(0, TILES, step, jnp.zeros((1, WAVES), F32))

    def far_field(waves):
        arrived = waves.finish()
        incoming = jnp.zeros((1, WAVES), F32)
        for c in range(BLOCKS):
            term = trans_ref[c : c + 1, :] * arrived[c : c + 1, :]
            incoming = incoming + jnp.where(b == c, jnp.zeros_like(term), term)

        @pl.loop(0, TILES)
        def _(tile):
            rows = rows_of(tile)
            spread = (cosine[rows, :] * incoming).astype(BF16)
            base[rows, :] = jnp.dot(spread, wave_in[...], preferred_element_type=F32)

    def fetch(tile, gbuf):
        for k in range(PER_ROW):

            @pl.loop(0, TILE // UNROLL)
            def _(turn):
                begin = k * ROWS + tile * TILE + turn * UNROLL
                values = [gbuf[places[begin + step]].astype(F32) for step in range(UNROLL)]
                for step, value in enumerate(values):
                    picked[pl.ds((begin + step) * 2, 2), :] = value

    def fields(tile):
        start = tile * TILE
        near = jnp.zeros((TILE, COEF), F32)
        for k in range(PER_ROW):
            low = picked[pl.ds(2 * (k * ROWS + start), TILE, 2), :]
            high = picked[pl.ds(2 * (k * ROWS + start) + 1, TILE, 2), :]
            wanted = jnp.concatenate([low, high], axis=1).astype(BF16)
            table = ids[pl.ds(k * ROWS + start, TILE), :]
            table = jnp.concatenate([table, table], axis=1).astype(BF16)
            term = jnp.zeros((TILE, COEF), F32)
            for t in range(TABLES):
                chosen = jnp.where(table == jnp.asarray(t, BF16), wanted, jnp.zeros_like(wanted))
                term = term + jnp.dot(chosen, padded[t], preferred_element_type=F32)
            near = near + term.astype(BF16).astype(F32)
        rows = rows_of(tile)
        return mie[rows, 0:COEF] * (near + base[rows, :])

    def widened(block):
        return jnp.concatenate([block, jnp.zeros((TILE, 256 - COEF), F32)], axis=1)

    loads[0].wait()

    @pl.loop(0, TILES)
    def _(tile):
        rows = rows_of(tile)
        cosine[rows, :] = jnp.cos(angle[rows, :].astype(F32))

    loads[1].wait()
    waves_first.start(own_wave())
    first.level_one()
    for load in loads[2:]:
        load.wait()
    wave_in[...] = jnp.concatenate(
        [wave_in_tall[...].astype(F32), jnp.zeros((256 - COEF, WAVES), F32)], axis=0
    ).T[:, 0:COEF].astype(BF16)
    far_field(waves_first)
    padded[...] = jnp.zeros_like(padded)
    for t in range(TABLES):
        padded[t, 0:COEF, :] = tables[t]
    for tile in range(TILES):
        mie[rows_of(tile), :] = turned(mie_tall[:, tile * TILE : (tile + 1) * TILE])
    for k in range(PER_ROW):

        @pl.loop(0, ROWS // UNROLL)
        def _(turn):
            for step in range(UNROLL):
                row = turn * UNROLL + step
                request = row * PER_ROW + k
                places[k * ROWS + row] = owners[request] * ROWS + near_rows[request]
                value = jnp.full((1, 128), table_ids[request], jnp.int32).astype(F32)
                ids[pl.ds(k * ROWS + row, 1), :] = value

    def square(cols, sums):
        u = u_ref[:, cols]
        return (sums[0] + total(u * u),)

    (squares,) = tall_sums(square, 1)
    first.level_two()
    first.level_three()
    first.finish()

    for tile in range(TILES):
        fetch(tile, gbuf_a)
        block = widened(fields(tile))
        narrow = block.astype(BF16)
        coded[rows_of(tile), :] = narrow
        second.store(tile, narrow)
        second.start(tile)
        b1_tall[:, tile * TILE : (tile + 1) * TILE] = block.T[0:COEF]

    b1_out = pltpu.make_async_copy(b1_tall, b1_hbm, out_sems.at[0])
    b1_out.start()
    waves_second.start(own_wave())

    def product(cols, sums):
        return (sums[0] + total(u_ref[:, cols] * b1_tall[:, cols]),)

    (inner,) = tall_sums(product, 1)
    slope = inner / jnp.maximum(squares, 1e-30)

    def left_over(cols, sums):
        rest = b1_tall[:, cols] - slope * u_ref[:, cols]
        return (sums[0] + total(rest * rest),)

    (left,) = tall_sums(left_over, 1)
    share_a.start(row_of(squares, inner, left, slope))
    second.level_one()
    share_b.start(row_of(*spread_stats(share_a.finish())))
    far_field(waves_second)
    second.level_two()
    squares, inner, left, slope = spread_stats(share_b.finish())
    beta_squared = squares + epsilon
    beta = jnp.sqrt(beta_squared)
    h11 = (squares - inner) / beta_squared
    rest_first = (inner + epsilon) / beta_squared
    gap = slope - rest_first
    h21 = jnp.sqrt((left + gap * gap * squares) / beta_squared + epsilon)
    scale = 1.0 / (beta * h21)
    second.level_three()
    first.drain()
    second.finish()

    sums = (jnp.zeros((1, 1), F32),) * 5
    for tile in range(TILES):
        fetch(tile, gbuf_b)
        q = widened(fields(tile)).T[0:COEF]
        cols = slice(tile * TILE, (tile + 1) * TILE)
        q_tall[:, cols] = q
        u, b1 = u_ref[:, cols], b1_tall[:, cols]
        v = (rest_first * u - b1) * scale
        w = (rest_first * (u - b1) - (b1 - q)) * scale
        pairs = (u * w, v * w, w * w, u * v, v * v)
        sums = tuple(have + total(pair) for have, pair in zip(sums, pairs))

    share_c.start(row_of(*sums))
    q_out = pltpu.make_async_copy(q_tall, q_hbm, out_sems.at[1])
    q_out.start()
    share_d.start(jnp.sum(share_c.finish(), axis=0, keepdims=True))
    second.drain()
    parts = jnp.sum(share_d.finish(), axis=0, keepdims=True)
    uw, vw, ww, uv, vv = (column(parts, place) for place in range(5))
    h12 = uw / beta
    h22 = vw
    left = ww + h12 * h12 * (squares / beta_squared - 2.0) + h22 * h22 * (vv - 2.0) + 2.0 * h12 * h22 * (uv / beta)
    h32 = jnp.sqrt(jnp.maximum(left, 0.0) + epsilon)
    gram_aa = h11 * h11 + h21 * h21
    gram_ab = h11 * h12 + h21 * h22
    gram_bb = h12 * h12 + h22 * h22 + h32 * h32
    rhs_first = beta * h11
    rhs_second = beta * h12
    determinant = gram_aa * gram_bb - gram_ab * gram_ab
    y1 = (gram_bb * rhs_first - gram_ab * rhs_second) / determinant
    y2 = (gram_aa * rhs_second - gram_ab * rhs_first) / determinant
    scal_ref[...] = row_of(y1 / beta, y2 * scale, rest_first)
    at_row = lax.broadcasted_iota(jnp.int32, (2, 3), 1)
    at_col = lax.broadcasted_iota(jnp.int32, (2, 3), 0)
    left_col = jnp.where(at_row == 0, h11, jnp.where(at_row == 1, h21, jnp.zeros((2, 3), F32)))
    right_col = jnp.where(at_row == 0, h12, jnp.where(at_row == 1, h22, h32))
    hess_ref[...] = jnp.where(at_col == 0, left_col, right_col)
    b1_out.wait()
    q_out.wait()


def body(incident, mie_coef, owner_dev, near_row, table_id, tables, wave_out, wave_in, plane_angle, far_trans):
    vmem = pl.BlockSpec(memory_space=pltpu.VMEM)
    smem = pl.BlockSpec(memory_space=pltpu.SMEM)
    anywhere = pl.BlockSpec(memory_space=pl.ANY)
    dma = pltpu.SemaphoreType.DMA
    u = incident[0].T
    blk_sems = [dma((BLOCKS - 1,)), dma((BLOCKS,))]
    grp_sems = [dma((GROUP - 1,)), dma((GROUP,))]
    b1, q, scal, hess = pl.pallas_call(
        kernel,
        out_shape=(
            jax.ShapeDtypeStruct((COEF, ROWS), F32),
            jax.ShapeDtypeStruct((COEF, ROWS), F32),
            jax.ShapeDtypeStruct((1, 128), F32),
            jax.ShapeDtypeStruct((2, 3), F32),
        ),
        in_specs=[smem, smem, smem, vmem] + [anywhere] * 5 + [vmem],
        out_specs=(anywhere, anywhere, vmem, vmem),
        scratch_shapes=[
            pltpu.VMEM((GROUP * ROWS, 2, 128), BF16),
            pltpu.VMEM((GROUP * ROWS, 2, 128), BF16),
            pltpu.SMEM((PER_ROW * ROWS,), jnp.int32),
            pltpu.VMEM((PER_ROW * ROWS * 2, 128), F32),
            pltpu.VMEM((PER_ROW * ROWS, 128), F32),
            pltpu.VMEM((TABLES, 256, COEF), BF16),
            pltpu.VMEM((ROWS, WAVES), F32),
            pltpu.VMEM((ROWS, COEF), F32),
            pltpu.VMEM((ROWS, 256), BF16),
            pltpu.VMEM((ROWS, 256), F32),
            pltpu.VMEM((COEF, ROWS), F32),
            pltpu.VMEM((TABLES, COEF, COEF), BF16),
            pltpu.VMEM((COEF, WAVES), BF16),
            pltpu.VMEM((WAVES, COEF), BF16),
            pltpu.VMEM((COEF, WAVES), BF16),
            pltpu.VMEM((ROWS, WAVES), BF16),
            pltpu.VMEM((COEF, ROWS), F32),
            pltpu.VMEM((COEF, ROWS), F32),
            pltpu.VMEM((BLOCKS, 1, WAVES), F32),
            pltpu.VMEM((BLOCKS, 1, WAVES), F32),
            pltpu.VMEM((GROUP, 1, 128), F32),
            pltpu.VMEM((BLOCKS, 1, 128), F32),
            pltpu.VMEM((GROUP, 1, 128), F32),
            pltpu.VMEM((BLOCKS, 1, 128), F32),
            dma((5,)),
            dma((2,)),
            dma((SENDS,)),
            dma((GROUP, CHUNKS)),
            dma((SENDS,)),
            dma((GROUP, CHUNKS)),
            *blk_sems,
            *blk_sems,
            *grp_sems,
            *blk_sems,
            *grp_sems,
            *blk_sems,
        ],
        compiler_params=pltpu.CompilerParams(
            collective_id=0, has_side_effects=True, vmem_limit_bytes=56 * 2**20
        ),
    )(
        owner_dev[0, :, 0],
        near_row[0],
        table_id[0],
        u,
        mie_coef[0].T,
        tables,
        wave_out,
        wave_in.T,
        plane_angle[0],
        far_trans[0, 0],
    )
    y1, y2, rest_first = scal[0, 0], scal[0, 1], scal[0, 2]
    sol = y1 * u + y2 * (rest_first * u - b1)
    res = u - y1 * (u - b1) - y2 * (rest_first * (u - b1) - (b1 - q))
    return sol.T[None], res.T[None], hess.T


def solution(mesh):
    return jax.shard_map(
        body,
        mesh=mesh,
        in_specs=(
            P("blk", "grp", None),
            P("blk", "grp", None),
            P("blk", "grp", None),
            P("blk", "grp"),
            P("blk", "grp"),
            P(),
            P(),
            P(),
            P("blk", "grp", None),
            P("blk", "grp", None, None),
        ),
        out_specs=(P("blk", "grp", None), P("blk", "grp", None), P()),
        check_vma=False,
    )
```

time: 126 us -> 108 us (0.86)
  Pallas kernels: 114 us -> 99.2 us
  local copies, waits for them, and re-layouts: 10.2 us -> 2.43 us
  other arithmetic: 1.33 us -> 5.14 us
    pallas_call x1, Pallas kernels: 114 us -> 99.2 us  [body(): pl.pallas_call(kernel, out_shape=(jax.ShapeDtypeStruct((COEF, ROWS), F32)...]
    unnamed x14 -> x7, local copies, waits for them, and re-layouts: 10.2 us -> 1.83 us
    broadcast_in_dim x0 -> x1, other arithmetic: none -> 5.14 us  [body(): return (sol.T[None], res.T[None], hess.T)]
where the time goes in v2:
time: 108 us; the launch traced here: 107 us
  Pallas kernels  99.2 us (92%)
  other arithmetic  5.14 us (5%)
  local copies, waits for them, and re-layouts  2.43 us (2%)
    pallas_call x1, Pallas kernels, body(): pl.pallas_call(kernel, out_shape=(jax.ShapeDtypeStruct((COEF, ROWS), F32)...  99.2 us
    broadcast_in_dim x1, other arithmetic, body(): return (sol.T[None], res.T[None], hess.T)  5.14 us

profile of v2, /device:TPU:0, one launch (start us, length us, event | category | flops | bytes accessed | tf_op | source)
XLA Modules:
  0.0 107.4 jit_solution(4567291871782770300)
XLA Ops:
  0.6 0.0 copy-start
  0.6 99.2 %shard_map.121 = (f32[240,1024]{1,0:T(8,128)}, f32[240,1024]{1,0:T(8,128)}, f32[1,128]{1,0:T(1,128)}, f32[2,3]{1,0:T(2,128)}) custom-call(s32[3072]{0:T(1024)} %bitcast.31, s32[3072]{0:T(1024)} %bitcast.32, s32[3072]{0:T(1024)} %bitcast.33, f32[240,1024]{1,0:T(8,128)} %bitcast.26, f32[240,1024]{1,0:T(8,128)} %bitcast.28, bf16[8,240,240]{2,1,0:T(8,128)(2,1)} %tables_hbm.1, ...), custom_call_target="tpu_custom_call" | custom-call | tf_op jit(solution)/shard_map/pallas_call | solution.py:471
  99.8 0.0 copy-start.1
  99.8 0.6 copy-done.1
  100.4 0.6 fusion
  101.0 0.0 copy-done
  101.0 5.1 %subtract_bitcast_fusion = (f32[1,1024,240]{1,2,0:T(8,128)}, f32[1,1024,240]{1,2,0:T(8,128)}) fusion(f32[240,1024]{1,0:T(8,128)} %get-tuple-element.8, f32[240,1024]{1,0:T(8,128)} %get-tuple-element.9, f32[]{:T(128)} %bitcast.12, f32[]{:T(128)} %bitcast.11, f32[]{:T(128)} %bitcast.10, f32[1,1024,240]{1,2,0:T(8,128)S(1)} %copy-done), kind=kLoop, calls=%fused_computation | loop fusion | flops 3194880 | bytes 4915212 | tf_op jit(solution)/shard_map/broadcast_in_dim | solution.py:537
  106.2 0.0 copy-start.2
  106.2 0.7 copy-done.2
  106.9 0.6 copy.14
Async XLA Ops:
  0.6 100.4 %copy-start = (f32[1,1024,240]{1,2,0:T(8,128)S(1)}, f32[1,1024,240]{1,2,0:T(8,128)}, u32[]{:S(2)}) copy-start(f32[1,1024,240]{1,2,0:T(8,128)} %param.10) | copy-start | bytes 2949124
  99.8 0.6 copy-start.1
  106.2 0.7 copy-start.2

commit v3 on v2

--- a/solution.py
+++ b/solution.py
@@ -20,14 +20,14 @@
 PER_ROW = 3
 GROUP = 16
 BLOCKS = 8
-CHUNKS = 16
-CHUNK = ROWS // CHUNKS
 TILE = 256
 TILES = ROWS // TILE
 UNROLL = 32
 
-Z_FIRST = (True, False, True, False, True, False, True, False, True, False, True, False, True, False, True, True)
-GO_RIGHT = (True, True, False, False, True, True, False, False, True, True, False, False, True, False, False, True)
+CHUNKS = 2 * TILES
+CHUNK_ROWS = tuple((tile * TILE + half * 144, (144, 112)[half]) for tile in range(TILES) for half in range(2))
+Z_FIRST = (True, False) * TILES
+GO_RIGHT = (True, True, False, False) * (TILES // 2)
 
 
 class Gather:
@@ -46,7 +46,8 @@
         return ((self.z + dz) % 2) * 8 + ((self.y + dy) % 4) * 2 + (self.c + dc) % 2
 
     def copy(self, origin, chunk, device, slot):
-        rows = pl.ds(pl.multiple_of(origin * ROWS + chunk * CHUNK, CHUNK), CHUNK)
+        begin, count = CHUNK_ROWS[chunk]
+        rows = pl.ds(origin * ROWS + begin, count)
         return pltpu.make_async_remote_copy(
             src_ref=self.gbuf.at[rows],
             dst_ref=self.gbuf.at[rows],
@@ -70,7 +71,7 @@
         self.gbuf[pl.ds(start, TILE)] = coded.reshape(TILE, 2, 128)
 
     def start(self, tile):
-        for k in range(tile * TILE // CHUNK, (tile + 1) * TILE // CHUNK):
+        for k in (2 * tile, 2 * tile + 1):
             self.send(self.me, k, self.right, self.left, self.across, self.partner)
 
     def level_one(self):
@@ -178,29 +179,40 @@
     return pl.ds(pl.multiple_of(tile * TILE, TILE), TILE)
 
 
+def cols_of(tile):
+    return slice(tile * TILE, (tile + 1) * TILE)
+
+
 def turned(tall):
     return jnp.concatenate([tall, jnp.zeros((256 - COEF, TILE), tall.dtype)], axis=0).T
 
 
 def kernel(
-    owners,
-    near_rows,
-    table_ids,
-    u_ref,
+    owners_hbm,
+    near_rows_hbm,
+    table_ids_hbm,
+    u_hbm,
     mie_hbm,
     tables_hbm,
     wave_out_hbm,
     wave_in_hbm,
     angle_hbm,
-    trans_ref,
+    trans_hbm,
     b1_hbm,
     q_hbm,
     scal_ref,
     hess_ref,
     gbuf_a,
     gbuf_b,
+    owners,
+    near_rows,
+    table_ids,
+    u_ref,
+    trans_ref,
     places,
-    picked,
+    picked_a,
+    picked_b,
+    ids_wide,
     ids,
     padded,
     cosine,
@@ -221,6 +233,7 @@
     stats_b,
     stats_c,
     stats_d,
+    u_sems,
     in_sems,
     out_sems,
     aga_send,
@@ -248,6 +261,12 @@
     for step in range(1, BLOCKS):
         pl.semaphore_signal(barrier, inc=1, device_id={"blk": (b + step) % BLOCKS}, device_id_type=MESH)
 
+    tall_loads = [
+        pltpu.make_async_copy(u_hbm.at[:, cols_of(tile)], u_ref.at[:, cols_of(tile)], u_sems.at[tile])
+        for tile in range(TILES)
+    ]
+    for load in tall_loads:
+        load.start()
     loads = [
         pltpu.make_async_copy(source, target, in_sems.at[place])
         for place, (source, target) in enumerate(
@@ -257,6 +276,10 @@
                 (wave_in_hbm, wave_in_tall),
                 (mie_hbm, mie_tall),
                 (tables_hbm, tables),
+                (trans_hbm, trans_ref),
+                (owners_hbm, owners),
+                (near_rows_hbm, near_rows),
+                (table_ids_hbm, table_ids),
             )
         )
     ]
@@ -273,7 +296,8 @@
     share_d = Share(stats_d, d_send, d_recv, "blk", BLOCKS)
 
     for tile in range(TILES):
-        block = turned(u_ref[:, tile * TILE : (tile + 1) * TILE]).astype(BF16)
+        tall_loads[tile].wait()
+        block = turned(u_ref[:, cols_of(tile)]).astype(BF16)
         coded[rows_of(tile), :] = block
         first.store(tile, block)
         if tile == 0:
@@ -283,7 +307,7 @@
     def tall_sums(step, count):
         sums = (jnp.zeros((1, 1), F32),) * count
         for tile in range(TILES):
-            sums = step(slice(tile * TILE, (tile + 1) * TILE), sums)
+            sums = step(cols_of(tile), sums)
         return sums
 
     def own_wave():
@@ -307,32 +331,37 @@
             spread = (cosine[rows, :] * incoming).astype(BF16)
             base[rows, :] = jnp.dot(spread, wave_in[...], preferred_element_type=F32)
 
-    def fetch(tile, gbuf):
-        for k in range(PER_ROW):
-
-            @pl.loop(0, TILE // UNROLL)
-            def _(turn):
-                begin = k * ROWS + tile * TILE + turn * UNROLL
-                values = [gbuf[places[begin + step]].astype(F32) for step in range(UNROLL)]
-                for step, value in enumerate(values):
-                    picked[pl.ds((begin + step) * 2, 2), :] = value
-
-    def fields(tile):
-        start = tile * TILE
+    def fields(gbuf, use):
+        buffers = (picked_a, picked_b)
+        blocks = [(tile, k) for tile in range(TILES) for k in range(PER_ROW)]
+
+        def fetch(place, turn):
+            tile, k = blocks[place]
+            begin = k * ROWS + tile * TILE + turn * UNROLL
+            values = [gbuf[places[begin + step]].astype(F32) for step in range(UNROLL)]
+            for step, value in enumerate(values):
+                buffers[place % 2][pl.ds((turn * UNROLL + step) * 2, 2), :] = value
+
+        for turn in range(TABLES):
+            fetch(0, turn)
         near = jnp.zeros((TILE, COEF), F32)
-        for k in range(PER_ROW):
-            low = picked[pl.ds(2 * (k * ROWS + start), TILE, 2), :]
-            high = picked[pl.ds(2 * (k * ROWS + start) + 1, TILE, 2), :]
+        for place, (tile, k) in enumerate(blocks):
+            low = buffers[place % 2][pl.ds(0, TILE, 2), :]
+            high = buffers[place % 2][pl.ds(1, TILE, 2), :]
             wanted = jnp.concatenate([low, high], axis=1).astype(BF16)
-            table = ids[pl.ds(k * ROWS + start, TILE), :]
-            table = jnp.concatenate([table, table], axis=1).astype(BF16)
+            table = ids[pl.ds(k * ROWS + tile * TILE, TILE), :]
+            table = jnp.concatenate([table, table], axis=1)
             term = jnp.zeros((TILE, COEF), F32)
             for t in range(TABLES):
+                if place + 1 < len(blocks):
+                    fetch(place + 1, t)
                 chosen = jnp.where(table == jnp.asarray(t, BF16), wanted, jnp.zeros_like(wanted))
                 term = term + jnp.dot(chosen, padded[t], preferred_element_type=F32)
             near = near + term.astype(BF16).astype(F32)
-        rows = rows_of(tile)
-        return mie[rows, 0:COEF] * (near + base[rows, :])
+            if k == PER_ROW - 1:
+                rows = rows_of(tile)
+                use(tile, mie[rows, 0:COEF] * (near + base[rows, :]))
+                near = jnp.zeros((TILE, COEF), F32)
 
     def widened(block):
         return jnp.concatenate([block, jnp.zeros((TILE, 256 - COEF), F32)], axis=1)
@@ -357,7 +386,7 @@
     for t in range(TABLES):
         padded[t, 0:COEF, :] = tables[t]
     for tile in range(TILES):
-        mie[rows_of(tile), :] = turned(mie_tall[:, tile * TILE : (tile + 1) * TILE])
+        mie[rows_of(tile), :] = turned(mie_tall[:, cols_of(tile)])
     for k in range(PER_ROW):
 
         @pl.loop(0, ROWS // UNROLL)
@@ -367,7 +396,9 @@
                 request = row * PER_ROW + k
                 places[k * ROWS + row] = owners[request] * ROWS + near_rows[request]
                 value = jnp.full((1, 128), table_ids[request], jnp.int32).astype(F32)
-                ids[pl.ds(k * ROWS + row, 1), :] = value
+                ids_wide[pl.ds(k * ROWS + row, 1), :] = value
+
+    ids[...] = ids_wide[...].astype(BF16)
 
     def square(cols, sums):
         u = u_ref[:, cols]
@@ -378,14 +409,15 @@
     first.level_three()
     first.finish()
 
-    for tile in range(TILES):
-        fetch(tile, gbuf_a)
-        block = widened(fields(tile))
+    def use_first(tile, block):
+        block = widened(block)
         narrow = block.astype(BF16)
         coded[rows_of(tile), :] = narrow
         second.store(tile, narrow)
         second.start(tile)
-        b1_tall[:, tile * TILE : (tile + 1) * TILE] = block.T[0:COEF]
+        b1_tall[:, cols_of(tile)] = block.T[0:COEF]
+
+    fields(gbuf_a, use_first)
 
     b1_out = pltpu.make_async_copy(b1_tall, b1_hbm, out_sems.at[0])
     b1_out.start()
@@ -419,17 +451,19 @@
     first.drain()
     second.finish()
 
-    sums = (jnp.zeros((1, 1), F32),) * 5
-    for tile in range(TILES):
-        fetch(tile, gbuf_b)
-        q = widened(fields(tile)).T[0:COEF]
-        cols = slice(tile * TILE, (tile + 1) * TILE)
+    sums = [jnp.zeros((1, 1), F32)] * 5
+
+    def use_second(tile, block):
+        q = widened(block).T[0:COEF]
+        cols = cols_of(tile)
         q_tall[:, cols] = q
         u, b1 = u_ref[:, cols], b1_tall[:, cols]
         v = (rest_first * u - b1) * scale
         w = (rest_first * (u - b1) - (b1 - q)) * scale
-        pairs = (u * w, v * w, w * w, u * v, v * v)
-        sums = tuple(have + total(pair) for have, pair in zip(sums, pairs))
+        for place, pair in enumerate((u * w, v * w, w * w, u * v, v * v)):
+            sums[place] = sums[place] + total(pair)
+
+    fields(gbuf_b, use_second)
 
     share_c.start(row_of(*sums))
     q_out = pltpu.make_async_copy(q_tall, q_hbm, out_sems.at[1])
@@ -460,9 +494,18 @@
     q_out.wait()
 
 
+def combine(scal_ref, hess_in_ref, u_ref, b1_ref, q_ref, sol_ref, res_ref, hess_ref):
+    scal = scal_ref[...]
+    y1, y2, rest_first = (column(scal, place) for place in range(3))
+    u, b1 = u_ref[...], b1_ref[...]
+    sol_ref[...] = y1 * u + y2 * (rest_first * u - b1)
+    image = u - b1
+    res_ref[...] = u - y1 * image - y2 * (rest_first * image - (b1 - q_ref[...]))
+    hess_ref[...] = hess_in_ref[...]
+
+
 def body(incident, mie_coef, owner_dev, near_row, table_id, tables, wave_out, wave_in, plane_angle, far_trans):
     vmem = pl.BlockSpec(memory_space=pltpu.VMEM)
-    smem = pl.BlockSpec(memory_space=pltpu.SMEM)
     anywhere = pl.BlockSpec(memory_space=pl.ANY)
     dma = pltpu.SemaphoreType.DMA
     u = incident[0].T
@@ -476,14 +519,21 @@
             jax.ShapeDtypeStruct((1, 128), F32),
             jax.ShapeDtypeStruct((2, 3), F32),
         ),
-        in_specs=[smem, smem, smem, vmem] + [anywhere] * 5 + [vmem],
+        in_specs=[anywhere] * 10,
         out_specs=(anywhere, anywhere, vmem, vmem),
         scratch_shapes=[
             pltpu.VMEM((GROUP * ROWS, 2, 128), BF16),
             pltpu.VMEM((GROUP * ROWS, 2, 128), BF16),
             pltpu.SMEM((PER_ROW * ROWS,), jnp.int32),
-            pltpu.VMEM((PER_ROW * ROWS * 2, 128), F32),
+            pltpu.SMEM((PER_ROW * ROWS,), jnp.int32),
+            pltpu.SMEM((PER_ROW * ROWS,), jnp.int32),
+            pltpu.VMEM((COEF, ROWS), F32),
+            pltpu.VMEM((BLOCKS, WAVES), F32),
+            pltpu.SMEM((PER_ROW * ROWS,), jnp.int32),
+            pltpu.VMEM((TILE * 2, 128), F32),
+            pltpu.VMEM((TILE * 2, 128), F32),
             pltpu.VMEM((PER_ROW * ROWS, 128), F32),
+            pltpu.VMEM((PER_ROW * ROWS, 128), BF16),
             pltpu.VMEM((TABLES, 256, COEF), BF16),
             pltpu.VMEM((ROWS, WAVES), F32),
             pltpu.VMEM((ROWS, COEF), F32),
@@ -503,7 +553,8 @@
             pltpu.VMEM((BLOCKS, 1, 128), F32),
             pltpu.VMEM((GROUP, 1, 128), F32),
             pltpu.VMEM((BLOCKS, 1, 128), F32),
-            dma((5,)),
+            dma((TILES,)),
+            dma((9,)),
             dma((2,)),
             dma((SENDS,)),
             dma((GROUP, CHUNKS)),
@@ -531,9 +582,20 @@
         plane_angle[0],
         far_trans[0, 0],
     )
-    y1, y2, rest_first = scal[0, 0], scal[0, 1], scal[0, 2]
-    sol = y1 * u + y2 * (rest_first * u - b1)
-    res = u - y1 * (u - b1) - y2 * (rest_first * (u - b1) - (b1 - q))
+    strip = pl.BlockSpec((COEF, TILE), lambda tile: (0, tile))
+    whole_scal = pl.BlockSpec((1, 128), lambda tile: (0, 0))
+    whole_hess = pl.BlockSpec((2, 3), lambda tile: (0, 0))
+    sol, res, hess = pl.pallas_call(
+        combine,
+        grid=(TILES,),
+        out_shape=(
+            jax.ShapeDtypeStruct((COEF, ROWS), F32),
+            jax.ShapeDtypeStruct((COEF, ROWS), F32),
+            jax.ShapeDtypeStruct((2, 3), F32),
+        ),
+        in_specs=[whole_scal, whole_hess, strip, strip, strip],
+        out_specs=(strip, strip, whole_hess),
+    )(scal, hess, u, b1, q)
     return sol.T[None], res.T[None], hess.T
 
 

time: 108 us -> 97 us (0.90)
  other arithmetic: 5.14 us -> 0 us
  Pallas kernels: 99.2 us -> 96.1 us
  local copies, waits for them, and re-layouts: 2.43 us -> 0 us
    pallas_call x1, Pallas kernels: 99.2 us -> 91.8 us  [body(): pl.pallas_call(kernel, out_shape=(jax.ShapeDtypeStruct((COEF, ROWS), F32)...]
    broadcast_in_dim x1 -> x0, other arithmetic: 5.14 us -> none  [body(): return (sol.T[None], res.T[None], hess.T)]
    pallas_call x0 -> x1, Pallas kernels: none -> 4.32 us  [body(): pl.pallas_call(combine, grid=(TILES,), out_shape=(jax.ShapeDtypeStruct((C...]
    unnamed x7 -> x0, local copies, waits for them, and re-layouts: 1.83 us -> none
where the time goes in v3:
time: 97 us; the launch traced here: 96.8 us
  Pallas kernels  96.1 us (99%)
    pallas_call x1, Pallas kernels, body(): pl.pallas_call(kernel, out_shape=(jax.ShapeDtypeStruct((COEF, ROWS), F32)...  91.8 us
    pallas_call x1, Pallas kernels, body(): pl.pallas_call(combine, grid=(TILES,), out_shape=(jax.ShapeDtypeStruct((C...  4.32 us

profile of v3, /device:TPU:0, one launch (start us, length us, event | category | flops | bytes accessed | tf_op | source)
XLA Modules:
  0.0 96.8 jit_solution(3636720843509152329)
XLA Ops:
  0.6 91.8 %shard_map.121 = (f32[240,1024]{1,0:T(8,128)}, f32[240,1024]{1,0:T(8,128)}, f32[1,128]{1,0:T(1,128)}, f32[2,3]{1,0:T(2,128)}) custom-call(s32[3072]{0:T(1024)} %bitcast.25, s32[3072]{0:T(1024)} %bitcast.26, s32[3072]{0:T(1024)} %bitcast.27, f32[240,1024]{1,0:T(8,128)} %bitcast.19, f32[240,1024]{1,0:T(8,128)} %bitcast.22, bf16[8,240,240]{2,1,0:T(8,128)(2,1)} %tables_hbm.1, ...), custom_call_target="tpu_custom_call" | custom-call | tf_op jit(solution)/shard_map/pallas_call | solution.py:514
  92.4 4.3 %shard_map.122 = (f32[240,1024]{1,0:T(8,128)}, f32[240,1024]{1,0:T(8,128)}, f32[2,3]{1,0:T(2,128)}) custom-call(f32[1,128]{1,0:T(1,128)} %get-tuple-element.10.scal_ref, f32[2,3]{1,0:T(2,128)} %get-tuple-element.11.hess_in_ref, f32[240,1024]{1,0:T(8,128)} %bitcast.20, f32[240,1024]{1,0:T(8,128)} %get-tuple-element.12.b1_ref, f32[240,1024]{1,0:T(8,128)} %get-tuple-element.13.q_ref), custom_call_target="tpu_custom_call" | custom-call | tf_op jit(solution)/shard_map/pallas_call | solution.py:588

commit v4 on v3

--- a/solution.py
+++ b/solution.py
@@ -75,31 +75,42 @@
             self.send(self.me, k, self.right, self.left, self.across, self.partner)
 
     def level_one(self):
+        last_hops = []
         for k in range(CHUNKS):
-            extra = () if Z_FIRST[k] else (self.across,)
-            origin = self.place(0, 3)
-            self.wait(origin, k)
-            self.send(origin, k, *((self.right,) if GO_RIGHT[k] else ()), *extra, self.partner)
-            origin = self.place(0, 1)
-            self.wait(origin, k)
-            self.send(origin, k, *(() if GO_RIGHT[k] else (self.left,)), *extra, self.partner)
+            z_first, onward = Z_FIRST[k], self.right if GO_RIGHT[k] else self.left
+            for dy, from_behind in ((3, GO_RIGHT[k]), (1, not GO_RIGHT[k])):
+                origin = self.place(0, dy)
+                self.wait(origin, k)
+                if from_behind and z_first:
+                    last_hops.append((origin, k, onward))
+                elif from_behind:
+                    self.send(origin, k, onward)
+                self.send(origin, k, *(() if z_first else (self.across,)), self.partner)
             origin = self.place(1, 0)
             self.wait(origin, k)
-            self.send(origin, k, *((self.right, self.left) if Z_FIRST[k] else ()), self.partner)
+            if z_first:
+                self.send(origin, k, onward)
+                last_hops.append((origin, k, self.left if GO_RIGHT[k] else self.right))
+            self.send(origin, k, self.partner)
+        for origin, k, device in last_hops:
+            self.send(origin, k, device)
 
     def level_two(self):
+        self.ending = ending = []
         for k in range(CHUNKS):
-            origin = self.place(0, 2)
+            z_first, right = Z_FIRST[k], GO_RIGHT[k]
+            if z_first:
+                origin = self.place(1, 3 if right else 1)
+                ending += [(self.place(1, 1 if right else 3), k), (self.place(0, 2), k)]
+            else:
+                origin = self.place(0, 2)
+                ending += [(self.place(1, 3), k), (self.place(1, 1), k)]
             self.wait(origin, k)
-            self.send(origin, k, *(() if Z_FIRST[k] else (self.across,)), self.partner)
-            origin = self.place(1, 3)
+            self.send(origin, k, (self.right if right else self.left) if z_first else self.across, self.partner)
+    def level_three(self):
+        for origin, k in self.ending:
             self.wait(origin, k)
-            self.send(origin, k, *((self.right,) if Z_FIRST[k] and GO_RIGHT[k] else ()), self.partner)
-            origin = self.place(1, 1)
-            self.wait(origin, k)
-            self.send(origin, k, *((self.left,) if Z_FIRST[k] and not GO_RIGHT[k] else ()), self.partner)
-
-    def level_three(self):
+            self.send(origin, k, self.partner)
         for k in range(CHUNKS):
             origin = self.place(1, 2)
             self.wait(origin, k)
@@ -213,7 +224,7 @@
     picked_a,
     picked_b,
     ids_wide,
-    ids,
+    masks,
     padded,
     cosine,
     base,
@@ -233,6 +244,7 @@
     stats_b,
     stats_c,
     stats_d,
+    places_sem,
     u_sems,
     in_sems,
     out_sems,
@@ -337,8 +349,8 @@
 
         def fetch(place, turn):
             tile, k = blocks[place]
-            begin = k * ROWS + tile * TILE + turn * UNROLL
-            values = [gbuf[places[begin + step]].astype(F32) for step in range(UNROLL)]
+            begin = tile * TILE + turn * UNROLL
+            values = [gbuf[places[(begin + step) * PER_ROW + k]].astype(F32) for step in range(UNROLL)]
             for step, value in enumerate(values):
                 buffers[place % 2][pl.ds((turn * UNROLL + step) * 2, 2), :] = value
 
@@ -349,14 +361,14 @@
             low = buffers[place % 2][pl.ds(0, TILE, 2), :]
             high = buffers[place % 2][pl.ds(1, TILE, 2), :]
             wanted = jnp.concatenate([low, high], axis=1).astype(BF16)
-            table = ids[pl.ds(k * ROWS + tile * TILE, TILE), :]
-            table = jnp.concatenate([table, table], axis=1)
-            term = jnp.zeros((TILE, COEF), F32)
+            rows = pl.ds(k * ROWS + tile * TILE, TILE)
+            chosen = []
             for t in range(TABLES):
                 if place + 1 < len(blocks):
                     fetch(place + 1, t)
-                chosen = jnp.where(table == jnp.asarray(t, BF16), wanted, jnp.zeros_like(wanted))
-                term = term + jnp.dot(chosen, padded[t], preferred_element_type=F32)
+                mask = masks[t, rows, :]
+                chosen.append(wanted * jnp.concatenate([mask, mask], axis=1))
+            term = jnp.dot(jnp.concatenate(chosen, axis=1), padded[...], preferred_element_type=F32)
             near = near + term.astype(BF16).astype(F32)
             if k == PER_ROW - 1:
                 rows = rows_of(tile)
@@ -378,13 +390,17 @@
     first.level_one()
     for load in loads[2:]:
         load.wait()
+    owners[...] = owners[...] * ROWS + near_rows[...]
+    to_places = pltpu.make_async_copy(owners, places, places_sem)
+    to_places.start()
     wave_in[...] = jnp.concatenate(
         [wave_in_tall[...].astype(F32), jnp.zeros((256 - COEF, WAVES), F32)], axis=0
     ).T[:, 0:COEF].astype(BF16)
     far_field(waves_first)
+    first.level_two()
     padded[...] = jnp.zeros_like(padded)
     for t in range(TABLES):
-        padded[t, 0:COEF, :] = tables[t]
+        padded[t * 256 : t * 256 + COEF, :] = tables[t]
     for tile in range(TILES):
         mie[rows_of(tile), :] = turned(mie_tall[:, cols_of(tile)])
     for k in range(PER_ROW):
@@ -394,18 +410,22 @@
             for step in range(UNROLL):
                 row = turn * UNROLL + step
                 request = row * PER_ROW + k
-                places[k * ROWS + row] = owners[request] * ROWS + near_rows[request]
                 value = jnp.full((1, 128), table_ids[request], jnp.int32).astype(F32)
                 ids_wide[pl.ds(k * ROWS + row, 1), :] = value
 
-    ids[...] = ids_wide[...].astype(BF16)
+    @pl.loop(0, PER_ROW * TILES)
+    def _(part):
+        rows = rows_of(part)
+        table = ids_wide[rows, :]
+        for t in range(TABLES):
+            masks[t, rows, :] = jnp.where(table == float(t), 1.0, 0.0).astype(BF16)
 
     def square(cols, sums):
         u = u_ref[:, cols]
         return (sums[0] + total(u * u),)
 
     (squares,) = tall_sums(square, 1)
-    first.level_two()
+    to_places.wait()
     first.level_three()
     first.finish()
 
@@ -524,8 +544,8 @@
         scratch_shapes=[
             pltpu.VMEM((GROUP * ROWS, 2, 128), BF16),
             pltpu.VMEM((GROUP * ROWS, 2, 128), BF16),
-            pltpu.SMEM((PER_ROW * ROWS,), jnp.int32),
-            pltpu.SMEM((PER_ROW * ROWS,), jnp.int32),
+            pltpu.VMEM((PER_ROW * ROWS,), jnp.int32),
+            pltpu.VMEM((PER_ROW * ROWS,), jnp.int32),
             pltpu.SMEM((PER_ROW * ROWS,), jnp.int32),
             pltpu.VMEM((COEF, ROWS), F32),
             pltpu.VMEM((BLOCKS, WAVES), F32),
@@ -533,8 +553,8 @@
             pltpu.VMEM((TILE * 2, 128), F32),
             pltpu.VMEM((TILE * 2, 128), F32),
             pltpu.VMEM((PER_ROW * ROWS, 128), F32),
-            pltpu.VMEM((PER_ROW * ROWS, 128), BF16),
-            pltpu.VMEM((TABLES, 256, COEF), BF16),
+            pltpu.VMEM((TABLES, PER_ROW * ROWS, 128), BF16),
+            pltpu.VMEM((TABLES * 256, COEF), BF16),
             pltpu.VMEM((ROWS, WAVES), F32),
             pltpu.VMEM((ROWS, COEF), F32),
             pltpu.VMEM((ROWS, 256), BF16),
@@ -553,6 +573,7 @@
             pltpu.VMEM((BLOCKS, 1, 128), F32),
             pltpu.VMEM((GROUP, 1, 128), F32),
             pltpu.VMEM((BLOCKS, 1, 128), F32),
+            dma,
             dma((TILES,)),
             dma((9,)),
             dma((2,)),

time: 97 us -> 94.2 us (0.971)
  Pallas kernels: 96.1 us -> 93.3 us
    pallas_call x1, Pallas kernels: 91.8 us -> 89 us  [body(): pl.pallas_call(kernel, out_shape=(jax.ShapeDtypeStruct((COEF, ROWS), F32)...]
where the time goes in v4:
time: 94.2 us; the launch traced here: 94 us
  Pallas kernels  93.3 us (99%)
    pallas_call x1, Pallas kernels, body(): pl.pallas_call(kernel, out_shape=(jax.ShapeDtypeStruct((COEF, ROWS), F32)...  89 us
    pallas_call x1, Pallas kernels, body(): pl.pallas_call(combine, grid=(TILES,), out_shape=(jax.ShapeDtypeStruct((C...  4.32 us

profile of v4, /device:TPU:0, one launch (start us, length us, event | category | flops | bytes accessed | tf_op | source)
XLA Modules:
  0.0 94.0 jit_solution(17649687846977942361)
XLA Ops:
  0.6 89.0 %shard_map.121 = (f32[240,1024]{1,0:T(8,128)}, f32[240,1024]{1,0:T(8,128)}, f32[1,128]{1,0:T(1,128)}, f32[2,3]{1,0:T(2,128)}) custom-call(s32[3072]{0:T(1024)} %bitcast.25, s32[3072]{0:T(1024)} %bitcast.26, s32[3072]{0:T(1024)} %bitcast.27, f32[240,1024]{1,0:T(8,128)} %bitcast.19, f32[240,1024]{1,0:T(8,128)} %bitcast.22, bf16[8,240,240]{2,1,0:T(8,128)(2,1)} %tables_hbm.1, ...), custom_call_target="tpu_custom_call" | custom-call | tf_op jit(solution)/shard_map/pallas_call | solution.py:534
  89.7 4.3 %shard_map.122 = (f32[240,1024]{1,0:T(8,128)}, f32[240,1024]{1,0:T(8,128)}, f32[2,3]{1,0:T(2,128)}) custom-call(f32[1,128]{1,0:T(1,128)} %get-tuple-element.10.scal_ref, f32[2,3]{1,0:T(2,128)} %get-tuple-element.11.hess_in_ref, f32[240,1024]{1,0:T(8,128)} %bitcast.20, f32[240,1024]{1,0:T(8,128)} %get-tuple-element.12.b1_ref, f32[240,1024]{1,0:T(8,128)} %get-tuple-element.13.q_ref), custom_call_target="tpu_custom_call" | custom-call | tf_op jit(solution)/shard_map/pallas_call | solution.py:609

commit v5 on v4

--- a/solution.py
+++ b/solution.py
@@ -154,9 +154,11 @@
         for step in range(1, self.size):
             other = (self.slot + step) % self.size
             self.copy(other, other, step).wait_recv()
+        return self.buf[...].reshape(self.size, self.buf.shape[2])
+
+    def drain(self):
         for step in range(1, self.size):
             self.copy(self.slot, (self.slot + step) % self.size, step).wait_send()
-        return self.buf[...].reshape(self.size, self.buf.shape[2])
 
 
 def row_of(*values):
@@ -469,9 +471,11 @@
     scale = 1.0 / (beta * h21)
     second.level_three()
     first.drain()
+    for share in (waves_first, waves_second, share_a, share_b):
+        share.drain()
     second.finish()
 
-    sums = [jnp.zeros((1, 1), F32)] * 5
+    sums = [jnp.zeros((1, TILE), F32)] * 5
 
     def use_second(tile, block):
         q = widened(block).T[0:COEF]
@@ -481,11 +485,11 @@
         v = (rest_first * u - b1) * scale
         w = (rest_first * (u - b1) - (b1 - q)) * scale
         for place, pair in enumerate((u * w, v * w, w * w, u * v, v * v)):
-            sums[place] = sums[place] + total(pair)
+            sums[place] = sums[place] + jnp.sum(pair, axis=0, keepdims=True)
 
     fields(gbuf_b, use_second)
 
-    share_c.start(row_of(*sums))
+    share_c.start(row_of(*[jnp.sum(part, axis=1, keepdims=True) for part in sums]))
     q_out = pltpu.make_async_copy(q_tall, q_hbm, out_sems.at[1])
     q_out.start()
     share_d.start(jnp.sum(share_c.finish(), axis=0, keepdims=True))
@@ -512,6 +516,8 @@
     hess_ref[...] = jnp.where(at_col == 0, left_col, right_col)
     b1_out.wait()
     q_out.wait()
+    share_c.drain()
+    share_d.drain()
 
 
 def combine(scal_ref, hess_in_ref, u_ref, b1_ref, q_ref, sol_ref, res_ref, hess_ref):
@@ -603,12 +609,12 @@
         plane_angle[0],
         far_trans[0, 0],
     )
-    strip = pl.BlockSpec((COEF, TILE), lambda tile: (0, tile))
+    strip = pl.BlockSpec((COEF, ROWS // 2), lambda half: (0, half))
     whole_scal = pl.BlockSpec((1, 128), lambda tile: (0, 0))
     whole_hess = pl.BlockSpec((2, 3), lambda tile: (0, 0))
     sol, res, hess = pl.pallas_call(
         combine,
-        grid=(TILES,),
+        grid=(2,),
         out_shape=(
             jax.ShapeDtypeStruct((COEF, ROWS), F32),
             jax.ShapeDtypeStruct((COEF, ROWS), F32),

time: 94.2 us -> 92.9 us (0.986)
  Pallas kernels: 93.3 us -> 92.2 us
    pallas_call x1, Pallas kernels: 4.32 us -> 3.35 us  [body(): pl.pallas_call(combine, grid=(2,), out_shape=(jax.ShapeDtypeStruct((COEF,...]
where the time goes in v5:
time: 92.9 us; the launch traced here: 92.8 us
  Pallas kernels  92.2 us (99%)
    pallas_call x1, Pallas kernels, body(): pl.pallas_call(kernel, out_shape=(jax.ShapeDtypeStruct((COEF, ROWS), F32)...  88.8 us
    pallas_call x1, Pallas kernels, body(): pl.pallas_call(combine, grid=(2,), out_shape=(jax.ShapeDtypeStruct((COEF,...  3.35 us

profile of v5, /device:TPU:0, one launch (start us, length us, event | category | flops | bytes accessed | tf_op | source)
XLA Modules:
  0.0 92.8 jit_solution(7971527850696648902)
XLA Ops:
  0.6 88.8 %shard_map.121 = (f32[240,1024]{1,0:T(8,128)}, f32[240,1024]{1,0:T(8,128)}, f32[1,128]{1,0:T(1,128)}, f32[2,3]{1,0:T(2,128)}) custom-call(s32[3072]{0:T(1024)} %bitcast.25, s32[3072]{0:T(1024)} %bitcast.26, s32[3072]{0:T(1024)} %bitcast.27, f32[240,1024]{1,0:T(8,128)} %bitcast.19, f32[240,1024]{1,0:T(8,128)} %bitcast.22, bf16[8,240,240]{2,1,0:T(8,128)(2,1)} %tables_hbm.1, ...), custom_call_target="tpu_custom_call" | custom-call | tf_op jit(solution)/shard_map/pallas_call | solution.py:540
  89.5 3.4 %shard_map.122 = (f32[240,1024]{1,0:T(8,128)}, f32[240,1024]{1,0:T(8,128)}, f32[2,3]{1,0:T(2,128)}) custom-call(f32[1,128]{1,0:T(1,128)} %get-tuple-element.10.scal_ref, f32[2,3]{1,0:T(2,128)} %get-tuple-element.11.hess_in_ref, f32[240,1024]{1,0:T(8,128)} %bitcast.20, f32[240,1024]{1,0:T(8,128)} %get-tuple-element.12.b1_ref, f32[240,1024]{1,0:T(8,128)} %get-tuple-element.13.q_ref), custom_call_target="tpu_custom_call" | custom-call | tf_op jit(solution)/shard_map/pallas_call | solution.py:615

commit v6 on v5

--- a/solution.py
+++ b/solution.py
@@ -147,7 +147,7 @@
 
     def start(self, row):
         self.buf[pl.ds(self.slot, 1)] = row.reshape(1, 1, row.shape[1])
-        for step in range(1, self.size):
+        for step in sorted(range(1, self.size), key=lambda step: -min(step % (self.size // 2), -step % (self.size // 2))):
             self.copy(self.slot, (self.slot + step) % self.size, step).start()
 
     def finish(self):
@@ -475,7 +475,7 @@
         share.drain()
     second.finish()
 
-    sums = [jnp.zeros((1, TILE), F32)] * 5
+    sums = [jnp.zeros((1, TILE), F32)] * 3
 
     def use_second(tile, block):
         q = widened(block).T[0:COEF]
@@ -484,7 +484,7 @@
         u, b1 = u_ref[:, cols], b1_tall[:, cols]
         v = (rest_first * u - b1) * scale
         w = (rest_first * (u - b1) - (b1 - q)) * scale
-        for place, pair in enumerate((u * w, v * w, w * w, u * v, v * v)):
+        for place, pair in enumerate((u * w, v * w, w * w)):
             sums[place] = sums[place] + jnp.sum(pair, axis=0, keepdims=True)
 
     fields(gbuf_b, use_second)
@@ -495,7 +495,9 @@
     share_d.start(jnp.sum(share_c.finish(), axis=0, keepdims=True))
     second.drain()
     parts = jnp.sum(share_d.finish(), axis=0, keepdims=True)
-    uw, vw, ww, uv, vv = (column(parts, place) for place in range(5))
+    uw, vw, ww = (column(parts, place) for place in range(3))
+    uv = epsilon * (squares - inner) / beta_squared * scale
+    vv = (left + gap * gap * squares) * (scale * scale)
     h12 = uw / beta
     h22 = vw
     left = ww + h12 * h12 * (squares / beta_squared - 2.0) + h22 * h22 * (vv - 2.0) + 2.0 * h12 * h22 * (uv / beta)

time: 92.9 us -> 92.9 us (level)
  no operation moved by 1% of the time
where the time goes in v6:
time: 92.9 us; the launch traced here: 92.7 us
  Pallas kernels  92.1 us (99%)
    pallas_call x1, Pallas kernels, body(): pl.pallas_call(kernel, out_shape=(jax.ShapeDtypeStruct((COEF, ROWS), F32)...  88.7 us
    pallas_call x1, Pallas kernels, body(): pl.pallas_call(combine, grid=(2,), out_shape=(jax.ShapeDtypeStruct((COEF,...  3.35 us

profile of v6, /device:TPU:0, one launch (start us, length us, event | category | flops | bytes accessed | tf_op | source)
XLA Modules:
  0.0 92.7 jit_solution(11096704386640889356)
XLA Ops:
  0.6 88.7 %shard_map.121 = (f32[240,1024]{1,0:T(8,128)}, f32[240,1024]{1,0:T(8,128)}, f32[1,128]{1,0:T(1,128)}, f32[2,3]{1,0:T(2,128)}) custom-call(s32[3072]{0:T(1024)} %bitcast.25, s32[3072]{0:T(1024)} %bitcast.26, s32[3072]{0:T(1024)} %bitcast.27, f32[240,1024]{1,0:T(8,128)} %bitcast.19, f32[240,1024]{1,0:T(8,128)} %bitcast.22, bf16[8,240,240]{2,1,0:T(8,128)(2,1)} %tables_hbm.1, ...), custom_call_target="tpu_custom_call" | custom-call | tf_op jit(solution)/shard_map/pallas_call | solution.py:542
  89.4 3.4 %shard_map.122 = (f32[240,1024]{1,0:T(8,128)}, f32[240,1024]{1,0:T(8,128)}, f32[2,3]{1,0:T(2,128)}) custom-call(f32[1,128]{1,0:T(1,128)} %get-tuple-element.10.scal_ref, f32[2,3]{1,0:T(2,128)} %get-tuple-element.11.hess_in_ref, f32[240,1024]{1,0:T(8,128)} %bitcast.20, f32[240,1024]{1,0:T(8,128)} %get-tuple-element.12.b1_ref, f32[240,1024]{1,0:T(8,128)} %get-tuple-element.13.q_ref), custom_call_target="tpu_custom_call" | custom-call | tf_op jit(solution)/shard_map/pallas_call | solution.py:617
